TPU v7x, 32 devices: a whole 2x2x4 slice. The times are simulated.
32 devices in a mesh: space: 4 (over y, core), vel: 8 (over z, x).
Axes of the slice: x: 2, y: 2, z: 4, core: 2. Of those that a mesh axis runs over, the one named last changes fastest.
Arguments:
- distribution: float32 [4, 256, 13824], P('space', None, 'vel'), may hold values from -6 to 6
- neighbours: int32 [4, 4], P('space'), may hold values from -1 to 3, as said below
- block_level: int32 [4], P('space'), may hold values from 0 to 2
- collide_mask: int32 [1024], P('space'), may hold values from 0 to 1, as said below
- gain_first: float32 [6, 13824], replicated, may hold values from -1.8 to 1.8
- gain_second: float32 [6, 13824], replicated, may hold values from -1.8 to 1.8
- loss_rates: float32 [13824], replicated, may hold values from 0.2 to 2
Outputs:
- distribution_next: float32 [4, 256, 13824], P('space', None, 'vel')
Inputs may be any that keep to these rules, and one draw needn't show every extreme that they name: `neighbours`: each entry is -1 or a block held by the same index of space as the block itself or by the index one below or one above (index s holds blocks s * 1 to (s + 1) - 1). `collide_mask`: the cells of one index of space (its 1 block) hold at most 128 ones, and some index holds exactly 128.
All inputs are finite; a program needn't handle non-finite values.
Results may differ from a plain program's by a relative error of at most 0.0003.
Values sent between devices are 32-bit elements; how exact they have to be, the bound alone decides.
A program may use at most 128 MiB of HBM per device.

v0:
```python
import functools

import jax
import jax.numpy as jnp
import numpy as np
from jax import lax
from jax.experimental import pallas as pl
from jax.experimental.pallas import tpu as pltpu
from jax.sharding import PartitionSpec as P

BSIDE = 16
VDIM = 24
ACT = 128
LANES = 128
GROUP = 8


weno_eps = 1e-06
courant = 0.2


def speed_rows(vel_start, vel_width):
    index = vel_start + jnp.arange(vel_width, dtype=jnp.int32)
    half = (VDIM - 1) / 2.0
    first = ((index // (VDIM * VDIM)).astype(jnp.float32) - half) / half
    second = ((index // VDIM % VDIM).astype(jnp.float32) - half) / half
    rows = [jnp.abs(first), jnp.abs(second), jnp.where(first < 0, 1.0, 0.0), jnp.where(second < 0, 1.0, 0.0)]
    return jnp.stack(rows + [jnp.zeros_like(first)] * 4)


def pack_strips(cells_ref, against_first, against_second, strips_ref):
    side = BSIDE

    def first(n):
        return cells_ref[n * side : (n + 1) * side]

    def second(n):
        return cells_ref[pl.ds(n, side, stride=side), :]

    at = 0
    for line, against in ((first, against_first), (second, against_second)):
        far = jnp.where(against, line(2), line(side - 3))
        for layer in (line(0), line(1), far, line(side - 2), line(side - 1)):
            strips_ref[at : at + side] = layer
            at += side


def sweep(line, against, speed, flux_ref):
    side = BSIDE

    def oriented(n):
        return jnp.where(against, line(side + 5 - n), line(n))

    values = [oriented(n) for n in range(4)]
    slopes = [values[n + 1] - values[n] for n in range(3)]
    bends = []
    for n in range(2):
        bend = slopes[n + 1] - slopes[n]
        bends.append(bend * bend * (13.0 / 3.0) + 4.0 * weno_eps)
    before = None
    for i in range(side + 1):
        values.append(oriented(i + 4))
        slopes.append(values[i + 4] - values[i + 3])
        bend = slopes[i + 3] - slopes[i + 2]
        bends.append(bend * bend * (13.0 / 3.0) + 4.0 * weno_eps)
        d0, d1, d2, d3 = slopes[i : i + 4]
        tilt_low = 3.0 * d1 - d0
        tilt_mid = d1 + d2
        tilt_high = d3 - 3.0 * d2
        rough_low = bends[i] + tilt_low * tilt_low
        rough_mid = bends[i + 1] + tilt_mid * tilt_mid
        rough_high = bends[i + 2] + tilt_high * tilt_high
        low2 = rough_low * rough_low
        mid2 = rough_mid * rough_mid
        high2 = rough_high * rough_high
        weight_low = mid2 * high2
        low3 = 3.0 * low2
        weight_mid = (low3 + low3) * high2
        weight_high = low3 * mid2
        guess_low = 5.0 * d1 - 2.0 * d0
        guess_mid = d1 + (d2 + d2)
        guess_high = 4.0 * d2 - d3
        above = weight_low * guess_low + weight_mid * guess_mid + weight_high * guess_high
        below = weight_low + weight_mid + weight_high
        edge = values[i + 2] + above / (6.0 * below)
        if before is not None:
            flux_ref[(i - 1) * side : i * side] = speed * (edge - before)
        before = edge


def advance(source_ref, ratio, u_ref, base_ref, left_ref, right_ref, speed_ref, out_ref, fluxes):
    side = BSIDE
    lanes = u_ref.shape[1]
    flux_one, flux_two, flux_turned = fluxes

    def first_line(n):
        return u_ref[n * side : (n + 1) * side]

    def second_line(n):
        return u_ref[pl.ds(n, side, stride=side), :]

    def ghost(face, block, own):
        at = block * side
        return (
            source_ref[3 * face] * left_ref[at : at + side]
            + source_ref[3 * face + 1] * own
            + source_ref[3 * face + 2] * right_ref[at : at + side]
        )

    def padded(line, faces, start):
        ghosts = {}
        for layer in range(3):
            ghosts[layer] = ghost(faces[0], start + 2 + layer, line(side - 3 + layer))
            ghosts[side + 3 + layer] = ghost(faces[1], start + layer, line(layer))
        return lambda n: ghosts[n] if n in ghosts else line(n - 3)

    against_first, against_second = against_masks(speed_ref)
    sweep(padded(first_line, (0, 1), 0), against_first, spread(speed_ref, 0), flux_one)
    sweep(padded(second_line, (2, 3), 5), against_second, spread(speed_ref, 1), flux_two)
    for n in range(side):
        back = side - 1 - n
        flux_turned[n * side : (n + 1) * side] = jnp.where(
            against_second, flux_two[back * side : (back + 1) * side], flux_two[n * side : (n + 1) * side]
        )
    for n in range(side):
        back = side - 1 - n
        rows = slice(n * side, (n + 1) * side)
        change = jnp.where(against_first, flux_one[back * side : (back + 1) * side], flux_one[rows])
        change = change + flux_turned[pl.ds(n, side, stride=side), :]
        moved = u_ref[rows] - ratio * change
        if base_ref is not None:
            moved = 0.5 * base_ref[rows] + 0.5 * moved
        out_ref[rows] = moved


def spread(speed_ref, row):
    return jnp.broadcast_to(speed_ref[row : row + 1], (BSIDE, speed_ref.shape[1]))


def against_masks(speed_ref):
    return spread(speed_ref, 2) > 0.5, spread(speed_ref, 3) > 0.5


def transport_kernel(
    source_ref, ratio_ref, u_ref, speed_ref, out_ref,
    one_ref, flux_one, flux_two, flux_turned,
    strips, from_left, from_right, sent_left, sent_right, got_left, got_right,
):
    tiles = u_ref.shape[0]
    me = lax.axis_index("space")
    count = lax.axis_size("space")
    has_left, has_right = me > 0, me < count - 1
    left, right = lax.rem(me + count - 1, count), lax.rem(me + 1, count)
    mesh_ids = pl.DeviceIdType.MESH
    ratio = ratio_ref[0]
    fluxes = (flux_one, flux_two, flux_turned)

    barrier = pltpu.get_barrier_semaphore()

    @pl.when(has_left)
    def _():
        pl.semaphore_signal(barrier, inc=1, device_id={"space": left}, device_id_type=mesh_ids)

    @pl.when(has_right)
    def _():
        pl.semaphore_signal(barrier, inc=1, device_id={"space": right}, device_id_type=mesh_ids)

    pl.semaphore_wait(barrier, has_left.astype(jnp.int32) + has_right.astype(jnp.int32))

    def to_right(turn, tile):
        return pltpu.make_async_remote_copy(
            src_ref=strips.at[turn, tile], dst_ref=from_left.at[turn, tile],
            send_sem=sent_right.at[turn, tile], recv_sem=got_left.at[turn, tile],
            device_id={"space": right}, device_id_type=mesh_ids,
        )

    def to_left(turn, tile):
        return pltpu.make_async_remote_copy(
            src_ref=strips.at[turn, tile], dst_ref=from_right.at[turn, tile],
            send_sem=sent_left.at[turn, tile], recv_sem=got_right.at[turn, tile],
            device_id={"space": left}, device_id_type=mesh_ids,
        )

    def send(turn, tile, cells_ref):
        pack_strips(cells_ref.at[tile], *against_masks(speed_ref.at[tile]), strips.at[turn, tile])

        @pl.when(has_right)
        def _():
            to_right(turn, tile).start()

        @pl.when(has_left)
        def _():
            to_left(turn, tile).start()

    def receive(turn, tile):
        @pl.when(has_left)
        def _():
            to_right(turn, tile).wait_recv()

        @pl.when(has_right)
        def _():
            to_left(turn, tile).wait_recv()

    def begin(tile, carry):
        send(0, tile, u_ref)
        return carry

    lax.fori_loop(0, tiles, begin, 0)

    @pl.when(me == 0)
    def _():
        from_left[...] = jnp.zeros_like(from_left)

    @pl.when(me == count - 1)
    def _():
        from_right[...] = jnp.zeros_like(from_right)

    def first(tile, carry):
        receive(0, tile)
        advance(
            source_ref, ratio, u_ref.at[tile], None, from_left.at[0, tile], from_right.at[0, tile],
            speed_ref.at[tile], one_ref.at[tile], fluxes,
        )
        send(1, tile, one_ref)
        return carry

    lax.fori_loop(0, tiles, first, 0)

    def second(tile, carry):
        receive(1, tile)
        advance(
            source_ref, ratio, one_ref.at[tile], u_ref.at[tile], from_left.at[1, tile], from_right.at[1, tile],
            speed_ref.at[tile], out_ref.at[tile], fluxes,
        )
        return carry

    lax.fori_loop(0, tiles, second, 0)

    def finish(tile, carry):
        for turn in range(2):

            @pl.when(has_right)
            def _():
                to_right(turn, tile).wait_send()

            @pl.when(has_left)
            def _():
                to_left(turn, tile).wait_send()

        return carry

    lax.fori_loop(0, tiles, finish, 0)


def transport(source, ratio, cells, speeds):
    tiles, count, lanes = cells.shape
    smem = pl.BlockSpec(memory_space=pltpu.SMEM)
    vmem = pl.BlockSpec(memory_space=pltpu.VMEM)
    strips = pltpu.VMEM((2, tiles, 10 * BSIDE, lanes), jnp.float32)
    return pl.pallas_call(
        transport_kernel,
        in_specs=[smem, smem, vmem, vmem],
        out_specs=vmem,
        out_shape=jax.ShapeDtypeStruct(cells.shape, jnp.float32),
        scratch_shapes=[pltpu.VMEM(cells.shape, jnp.float32)]
        + [pltpu.VMEM((count, lanes), jnp.float32)] * 3
        + [strips] * 3
        + [pltpu.SemaphoreType.DMA((2, tiles))] * 4,
        compiler_params=pltpu.CompilerParams(
            collective_id=0, has_side_effects=True, vmem_limit_bytes=48 * 1024 * 1024
        ),
    )(source, ratio, cells, speeds)


def tiled(rows):
    count, width = rows.shape
    tiles = pl.cdiv(width, LANES)
    rows = jnp.pad(rows, ((0, 0), (0, tiles * LANES - width)))
    return rows.reshape(count, tiles, LANES).transpose(1, 0, 2)


def lane_pieces(tiles, width):
    return [(t, t * LANES, min(width, (t + 1) * LANES)) for t in range(tiles)]


def gather_kernel(chosen_ref, cells_ref, out_ref, picked_ref, rows_ref):
    parts, planes, each, plane = out_ref.shape
    tiles = cells_ref.shape[0]

    def one(slot, carry):
        row = chosen_ref[slot]
        for tile in range(tiles):
            picked_ref[tile, pl.ds(slot, 1), :] = cells_ref[tile, pl.ds(row, 1), :]
        return carry

    lax.fori_loop(0, parts * each, one, 0, unroll=8)
    for tile in range(tiles):
        rows_ref[:, tile * LANES : (tile + 1) * LANES] = picked_ref[tile]
    for part in range(parts):
        for n in range(planes):
            out_ref[part, n] = rows_ref[part * each : (part + 1) * each, n * plane : (n + 1) * plane]


def gather(chosen, cells, shape):
    return pl.pallas_call(
        gather_kernel,
        in_specs=[pl.BlockSpec(memory_space=pltpu.SMEM), pl.BlockSpec(memory_space=pltpu.VMEM)],
        out_specs=pl.BlockSpec(memory_space=pltpu.VMEM),
        out_shape=jax.ShapeDtypeStruct(shape, jnp.float32),
        scratch_shapes=[
            pltpu.VMEM((cells.shape[0], shape[0] * shape[2], LANES), jnp.float32),
            pltpu.VMEM((shape[0] * shape[2], cells.shape[0] * LANES), jnp.float32),
        ],
    )(chosen, cells)


def scatter_kernel(chosen_ref, count_ref, cells_ref, change_ref, out_ref, rows_ref):
    parts, planes, each, plane = change_ref.shape
    for tile, begin, end in lane_pieces(cells_ref.shape[0], out_ref.shape[1]):
        out_ref[:, begin:end] = cells_ref[tile, :, : end - begin]
    for part in range(parts):
        for n in range(planes):
            rows_ref[part * each : (part + 1) * each, n * plane : (n + 1) * plane] = change_ref[part, n]

    def one(slot, carry):
        row = pl.ds(chosen_ref[slot], 1)
        out_ref[row, :] += rows_ref[pl.ds(slot, 1), :]
        return carry

    lax.fori_loop(0, count_ref[0], one, 0)


def scatter(chosen, count, cells, change):
    smem = pl.BlockSpec(memory_space=pltpu.SMEM)
    vmem = pl.BlockSpec(memory_space=pltpu.VMEM)
    parts, planes, each, plane = change.shape
    return pl.pallas_call(
        scatter_kernel,
        in_specs=[smem, smem, vmem, vmem],
        out_specs=vmem,
        out_shape=jax.ShapeDtypeStruct((cells.shape[1], planes * plane), jnp.float32),
        scratch_shapes=[pltpu.VMEM((parts * each, planes * plane), jnp.float32)],
    )(chosen, count, cells, change)


def halves(table):
    high = table.astype(jnp.bfloat16)
    low = (table - high.astype(jnp.float32)).astype(jnp.bfloat16)
    return high, low


def dot(left, right):
    return jnp.dot(left, right, preferred_element_type=jnp.float32)


def collision(values, tables, depth):
    first_ref, second_ref, loss_ref, plane_ref, line_ref = tables
    size, plane = values.shape
    group = size // depth

    def transforms(cubes):
        high, low = halves(jnp.concatenate(cubes, axis=0) if len(cubes) > 1 else cubes[0])
        rows = high.shape[0]
        wide = dot(jnp.concatenate([high, low], axis=0), plane_ref[0])
        mapped = wide[:rows] + (wide[rows:] + dot(high, plane_ref[1]))
        results = []
        for n in range(len(cubes)):
            high, low = halves(mapped[n * size : (n + 1) * size])
            wide = dot(line_ref[...], high)
            results.append(wide[:size] + (wide[size:] + dot(line_ref[:size], low)))
        return results

    spectrum = transforms([values])[0].reshape(depth, group, plane)

    def scaled(multiplier):
        return (spectrum * multiplier[:, None, :]).reshape(size, plane)

    total = -values * transforms([scaled(loss_ref[...])])[0]

    def one(term, total):
        image_one, image_two = transforms([scaled(first_ref[term]), scaled(second_ref[term])])
        return total + image_one * image_two

    return lax.fori_loop(0, first_ref.shape[0], one, total)


def collide_kernel(cells_ref, *refs):
    depth, group, plane = cells_ref.shape
    out_ref = refs[-1]
    total = collision(cells_ref[...].reshape(depth * group, plane), refs[:-1], depth)
    out_ref[...] = total.reshape(depth, group, plane)


def swap_collide_kernel(
    cells_ref, first_ref, second_ref, loss_ref, plane_ref, line_ref, out_ref,
    first_cube, second_cube, loss_cube,
    got, result, sent_in, got_in, own_in, sent_out, got_out, own_out,
):
    parts = lax.axis_size("vel")
    blocks, planes, group, plane = cells_ref.shape
    chunks = blocks // parts
    me = lax.axis_index("vel")
    mesh_ids = pl.DeviceIdType.MESH
    peers = [lax.rem(me + n, parts) for n in range(parts)]
    tables = (first_cube, second_cube, loss_cube, plane_ref, line_ref)

    barrier = pltpu.get_barrier_semaphore()
    for peer in peers[1:]:
        pl.semaphore_signal(barrier, inc=1, device_id={"vel": peer}, device_id_type=mesh_ids)
    pl.semaphore_wait(barrier, parts - 1)

    def swap(chunk, from_ref, to_ref, send_sem, recv_sem, own_sem):
        mine = chunk * parts + me
        copies = []
        for n, peer in enumerate(peers):
            source = from_ref.at[chunk * parts + peer]
            if n == 0:
                copies.append(pltpu.make_async_copy(source, to_ref.at[mine], own_sem.at[chunk]))
            else:
                copies.append(
                    pltpu.make_async_remote_copy(
                        src_ref=source, dst_ref=to_ref.at[mine],
                        send_sem=send_sem.at[chunk, n], recv_sem=recv_sem.at[chunk, n],
                        device_id={"vel": peer}, device_id_type=mesh_ids,
                    )
                )
            copies[-1].start()
        return copies

    incoming = [swap(chunk, cells_ref, got, sent_in, got_in, own_in) for chunk in range(chunks)]
    for row in range(parts * planes):
        columns = slice(row * plane, (row + 1) * plane)
        for term in range(first_ref.shape[0]):
            first_cube[term, row : row + 1, :] = first_ref[term : term + 1, columns]
            second_cube[term, row : row + 1, :] = second_ref[term : term + 1, columns]
        loss_cube[row : row + 1, :] = loss_ref[:, columns]
    outgoing = []
    for chunk in range(chunks):
        for copy in incoming[chunk][1:]:
            copy.wait_recv()
        incoming[chunk][0].wait()
        held = slice(chunk * parts, (chunk + 1) * parts)
        values = got[held].reshape(parts * planes * group, plane)
        result[held] = collision(values, tables, parts * planes).reshape(parts, planes, group, plane)
        outgoing.append(swap(chunk, result, out_ref, sent_out, got_out, own_out))
    for copies in outgoing:
        copies[0].wait()
        for copy in copies[1:]:
            copy.wait_recv()
    for copies in incoming + outgoing:
        for copy in copies[1:]:
            copy.wait_send()


def hartley_tables(vdim):
    index = np.arange(vdim, dtype=np.float64)
    angle = 2.0 * np.pi * np.outer(index, index) / vdim
    table = (np.cos(angle) + np.sin(angle)) / np.sqrt(vdim)

    def split(wide):
        wide = wide.astype(np.float32)
        high = wide.astype(jnp.bfloat16)
        return np.stack([high, (wide - high.astype(np.float32)).astype(jnp.bfloat16)])

    return split(np.kron(table, table)), np.concatenate(split(np.kron(table, np.eye(GROUP))))


def collision_operands(gain_first, gain_second, loss_rates):
    plane_table, line_table = hartley_tables(VDIM)
    return gain_first, gain_second, loss_rates[None], jnp.asarray(plane_table), jnp.asarray(line_table)


def collide(cells, operands):
    depth, count, plane = cells.shape
    gain_first, gain_second, loss_rates = operands[:3]
    cube = (gain_first.shape[0], depth, plane)
    operands = (gain_first.reshape(cube), gain_second.reshape(cube), loss_rates.reshape(cube[1:])) + operands[3:]
    spare = -count % GROUP
    if spare:
        cells = jnp.pad(cells, ((0, 0), (0, spare), (0, 0)))
    cell_spec = pl.BlockSpec((depth, GROUP, plane), lambda n: (0, n, 0))

    def whole(shape):
        return pl.BlockSpec(shape, lambda n: (0,) * len(shape))

    result = pl.pallas_call(
        collide_kernel,
        grid=((count + spare) // GROUP,),
        in_specs=[cell_spec] + [whole(array.shape) for array in operands],
        out_specs=cell_spec,
        out_shape=jax.ShapeDtypeStruct(cells.shape, jnp.float32),
        compiler_params=pltpu.CompilerParams(vmem_limit_bytes=56 * 1024 * 1024),
    )(cells, *operands)
    return result[:, :count]


def swap_collide(cells, operands):
    chunks, parts = cells.shape[0] // lax.axis_size("vel"), lax.axis_size("vel")
    vmem = pl.BlockSpec(memory_space=pltpu.VMEM)
    across = pltpu.SemaphoreType.DMA((chunks, parts))
    own = pltpu.SemaphoreType.DMA((chunks,))
    cube = (VDIM, cells.shape[3])
    gains = pltpu.VMEM((operands[0].shape[0],) + cube, jnp.float32)
    return pl.pallas_call(
        swap_collide_kernel,
        in_specs=[vmem] * (1 + len(operands)),
        out_specs=vmem,
        out_shape=jax.ShapeDtypeStruct(cells.shape, jnp.float32),
        scratch_shapes=[gains, gains, pltpu.VMEM(cube, jnp.float32)]
        + [pltpu.VMEM(cells.shape, jnp.float32)] * 2
        + [across, across, own] * 2,
        compiler_params=pltpu.CompilerParams(
            collective_id=1, has_side_effects=True, vmem_limit_bytes=56 * 1024 * 1024
        ),
    )(cells, *operands)


def shards(
    distribution, neighbours, block_level, collide_mask, gain_first, gain_second, loss_rates
):
    blocks, cell_count, width = distribution.shape
    assert blocks == 1
    density = distribution.reshape(cell_count, width)
    speeds = speed_rows(lax.axis_index("vel") * width, width)
    ratio = courant * jnp.exp2(block_level.astype(jnp.float32))
    offset = neighbours[0] - (lax.axis_index("space") - 1)
    source = (offset[:, None] == jnp.arange(3)) & (neighbours[0] >= 0)[:, None]
    source = source.astype(jnp.float32).reshape(-1)

    section_two = transport(source, ratio, tiled(density), tiled(speeds))

    parts = lax.axis_size("vel")
    each = ACT // parts
    cell_index = jnp.arange(cell_count)
    rank = jnp.sum(jnp.where(cell_index[:, None] < cell_index, collide_mask[:, None], 0), axis=0)
    hit = (rank[:, None] == jnp.arange(ACT)) & (collide_mask > 0)[:, None]
    chosen = jnp.sum(jnp.where(hit, cell_index[:, None], 0), axis=0)
    held = jnp.sum(collide_mask)[None]

    plane = VDIM * VDIM
    operands = collision_operands(gain_first, gain_second, loss_rates)
    if width % plane == 0 and each % GROUP == 0:
        sent = gather(chosen, section_two, (ACT // GROUP, width // plane, GROUP, plane))
        change = swap_collide(sent, operands)
    else:
        sent = gather(chosen, section_two, (parts, 1, each, width))
        got = lax.all_to_all(sent, "vel", split_axis=0, concat_axis=0, tiled=True)
        got = jnp.transpose(got.reshape(parts, each, width), (1, 0, 2))
        got = got.reshape(each, VDIM, plane).transpose(1, 0, 2)
        change = collide(got, operands).transpose(1, 0, 2).reshape(each, parts, width)
        change = change.transpose(1, 0, 2)[:, None]
        change = lax.all_to_all(change, "vel", split_axis=0, concat_axis=0, tiled=True)
    return scatter(chosen, held, section_two, change).reshape(blocks, cell_count, width)


def solution(mesh):
    in_specs = (P("space", None, "vel"), P("space", None), P("space"), P("space"), P(), P(), P())
    out_specs = P("space", None, "vel")
    return jax.shard_map(shards, mesh=mesh, in_specs=in_specs, out_specs=out_specs, check_vma=False)
```

profile of v0, /device:TPU:1, one launch (start us, length us, event | category | flops | bytes accessed | tf_op | source)
XLA Modules:
  0.0 106.0 jit_solution(9958064413084946315)
XLA Ops:
  0.7 1.3 %reduce_sum.29 = s32[]{:T(128)} reduce(s32[256]{0:T(256)} %param.12, s32[]{:T(128)} %constant.49.clone.1), dimensions={0}, to_apply=%region_2.3 | reduce | flops 255 | bytes 1032 | tf_op jit(solution)/shard_map/reduce_sum | solution.py:538
  2.0 0.7 subtract_bitcast_fusion
  2.7 0.7 compare_bitcast_fusion
  3.4 0.7 broadcast_compare_fusion
  4.0 0.1 fusion.8
  4.1 0.1 reshape.147.source_ref
  4.2 0.8 select_reduce_fusion
  5.0 0.7 select_reduce_fusion.1.chosen_ref
  5.7 0.1 fusion.5
  5.9 0.1 compare_select_fusion
  6.0 0.1 stack.5
  6.1 1.5 %broadcast_in_dim.54.loss_ref = f32[1,13824]{1,0:T(1,128)} reshape(f32[13824]{0:T(1024)} %param.15) | data formatting | bytes 110592 | tf_op jit(solution)/shard_map/broadcast_in_dim | solution.py:470
  7.6 2.8 %pad.8 = f32[256,1792]{0,1:T(8,128)} pad(f32[256,1728]{0,1:T(8,128)} %bitcast.16, f32[]{:T(128)} %constant.54.clone.1), padding=0_0x0_64 | pad | bytes 3604484 | tf_op jit(solution)/shard_map/jit(_pad)/pad | solution.py:278
  10.4 1.8 %copy.13 = f32[256,14,128]{2,0,1:T(8,128)S(1)} copy(f32[256,14,128]{0,2,1:T(8,128)} %bitcast.15) | data formatting | bytes 3670016 | tf_op jit(solution)/shard_map/reshape | solution.py:279
  12.2 30.7 %shard_map.91.cells_ref = f32[14,256,128]{2,1,0:T(8,128)S(1)} custom-call(f32[12]{0:T(128)S(1)} %reshape.147.source_ref, f32[1]{0:T(128)S(6)} %mul.6.ratio_ref, f32[14,256,128]{2,1,0:T(8,128)S(1)} %bitcast.13, f32[14,8,128]{2,1,0:T(8,128)S(1)} %pad_bitcast_fusion.speed_ref), custom_call_target="tpu_custom_call" | custom-call | tf_op jit(solution)/shard_map/pallas_call | solution.py:260
  42.9 0.0 copy-start
  43.0 1.2 %copy-done = f32[14,256,128]{2,1,0:T(8,128)} copy-done((f32[14,256,128]{2,1,0:T(8,128)}, f32[14,256,128]{2,1,0:T(8,128)S(1)}, u32[]{:S(2)}) %copy-start) | copy-done | bytes 1835032
  44.2 3.6 %shard_map.92.cells_ref = f32[16,3,8,576]{3,2,1,0:T(8,128)} custom-call(s32[128]{0:T(128)} %select_reduce_fusion.1.chosen_ref, f32[14,256,128]{2,1,0:T(8,128)} %copy-done), custom_call_target="tpu_custom_call" | custom-call | tf_op jit(solution)/shard_map/pallas_call | solution.py:305
  47.8 50.4 %shard_map.93.change_ref = f32[16,3,8,576]{3,2,1,0:T(8,128)} custom-call(f32[16,3,8,576]{3,2,1,0:T(8,128)} %shard_map.92.cells_ref, f32[6,13824]{1,0:T(8,128)} %first_ref.1, f32[6,13824]{1,0:T(8,128)} %second_ref.1, f32[1,13824]{1,0:T(1,128)} %broadcast_in_dim.54.loss_ref, bf16[2,576,576]{2,1,0:T(8,128)(2,1)} %constant.63.clone.plane_ref, ...), custom_call_target="tpu_custom_call" | custom-call | tf_op jit(solution)/shard_map/pallas_call | solution.py:504
  98.2 5.1 %shard_map.94 = f32[256,1728]{1,0:T(8,128)} custom-call(s32[128]{0:T(128)} %select_reduce_fusion.1.chosen_ref, s32[1]{0:T(128)} %bitcast.count_ref, f32[14,256,128]{2,1,0:T(8,128)} %copy-done, f32[16,3,8,576]{3,2,1,0:T(8,128)} %shard_map.93.change_ref), custom_call_target="tpu_custom_call" | custom-call | tf_op jit(solution)/shard_map/pallas_call | solution.py:337
  103.3 2.7 %copy.14 = f32[1,256,1728]{1,2,0:T(8,128)} copy(f32[1,256,1728]{2,1,0:T(8,128)} %bitcast.14) | data formatting | bytes 3538944 | tf_op jit(solution)/shard_map/reshape | solution.py:553
  (2 shorter events, 0.0 us)
Async XLA Ops:
  42.9 1.3 %copy-start = (f32[14,256,128]{2,1,0:T(8,128)}, f32[14,256,128]{2,1,0:T(8,128)S(1)}, u32[]{:S(2)}) copy-start(f32[14,256,128]{2,1,0:T(8,128)S(1)} %shard_map.91.cells_ref) | copy-start | bytes 5505028
where the time goes:
time: 108 us; the launch traced here: 106 us
  Pallas kernels  89.8 us (83%)
  local copies, waits for them, and re-layouts  10.2 us (9%)
  other arithmetic  5.2 us (5%)
    pallas_call x1, Pallas kernels, swap_collide(): pl.pallas_call(swap_collide_kernel, in_specs=[vmem] * (1 + len(operands))...  50.4 us
    pallas_call x1, Pallas kernels, transport(): pl.pallas_call(transport_kernel, in_specs=[smem, smem, vmem, vmem], out_s...  30.7 us
    pallas_call x1, Pallas kernels, scatter(): pl.pallas_call(scatter_kernel, in_specs=[smem, smem, vmem, vmem], out_spe...  5.06 us
    pallas_call x1, Pallas kernels, gather(): pl.pallas_call(gather_kernel, in_specs=[pl.BlockSpec(memory_space=pltpu.S...  3.62 us
    pad x1, local copies, waits for them, and re-layouts, tiled(): rows = jnp.pad(rows, ((0, 0), (0, tiles * LANES - width)))  2.85 us
    reshape x1, local copies, waits for them, and re-layouts, shards(): scatter(chosen, held, section_two, change)  2.7 us

commit v1 on v0

--- a/solution.py
+++ b/solution.py
@@ -515,11 +515,426 @@
     )(cells, *operands)
 
 
+def dht8(x):
+    e = [x[n] + x[n + 4] for n in range(4)]
+    o = [x[n] - x[n + 4] for n in range(4)]
+    a, b = e[0] + e[2], e[0] - e[2]
+    c, d = e[1] + e[3], e[1] - e[3]
+    p, q = o[0] + o[2], o[0] - o[2]
+    root = float(np.sqrt(2.0))
+    r, s = root * o[1], root * o[3]
+    return [a + c, p + r, b + d, q + s, a - c, p - r, b - d, q - s]
+
+
+def dht24(x):
+    plain, even, odd = [], [], []
+    for n in range(8):
+        x0, x1, x2 = x[(3 * n) % 24], x[(3 * n + 8) % 24], x[(3 * n + 16) % 24]
+        total = x1 + x2
+        plain.append(x0 + total)
+        even.append(x0 - 0.5 * total)
+        odd.append(float(np.sqrt(0.75)) * (x1 - x2))
+    plain, even, odd = dht8(plain), dht8(even), dht8(odd)
+    result = []
+    for f in range(24):
+        back = odd[-f % 8]
+        result.append((plain[f % 8], even[f % 8] + back, even[f % 8] - back)[f % 3])
+    return result
+
+
+LAG = 2
+
+
+def fused_kernel(
+    near_ref, level_ref, x_ref, mask_ref, first_ref, second_ref, loss_ref, plane_ref, speed_ref, out_ref,
+    u_ref, one_ref, two_ref, flux_one, flux_two, flux_turned, speeds, strips, from_left, from_right,
+    pick, spread_back, table, first_cube, second_cube, loss_cube, lhs, mapped, spectrum, total,
+    sent, got, result, back,
+    sent_left, sent_right, got_left, got_right, sent_in, got_in, own_in, sent_out, got_out, own_out,
+):
+    tiles, count, lanes = u_ref.shape
+    width = x_ref.shape[0]
+    parts, each, wide = got.shape
+    chunks = result.shape[0]
+    plane = VDIM * VDIM
+    planes = width // plane
+    terms = first_ref.shape[0]
+    me = lax.axis_index("vel")
+    row = lax.axis_index("space")
+    rows = lax.axis_size("space")
+    has_left, has_right = row > 0, row < rows - 1
+    left, right = lax.rem(row + rows - 1, rows), lax.rem(row + 1, rows)
+    peers = [lax.rem(me + n, parts) for n in range(parts)]
+    mesh_ids = pl.DeviceIdType.MESH
+    fluxes = (flux_one, flux_two, flux_turned)
+
+    barrier = pltpu.get_barrier_semaphore()
+
+    @pl.when(has_left)
+    def _():
+        pl.semaphore_signal(barrier, inc=1, device_id={"space": left}, device_id_type=mesh_ids)
+
+    @pl.when(has_right)
+    def _():
+        pl.semaphore_signal(barrier, inc=1, device_id={"space": right}, device_id_type=mesh_ids)
+
+    for peer in peers[1:]:
+        pl.semaphore_signal(barrier, inc=1, device_id={"vel": peer}, device_id_type=mesh_ids)
+
+    ratio = courant * jnp.left_shift(1, level_ref[0]).astype(jnp.float32)
+    source = []
+    for face in range(4):
+        for step in (-1, 0, 1):
+            held = (near_ref[face] == row + step) & (near_ref[face] >= 0)
+            source.append(jnp.where(held, 1.0, 0.0))
+
+    half = (VDIM - 1) / 2.0
+    start = (me * planes).astype(jnp.float32)
+    toward = (speed_ref[:, 0, :] + start - half) / half
+    across = speed_ref[:, 1, :]
+    for n, value in enumerate(
+        (jnp.abs(toward), jnp.abs(across), jnp.where(toward < 0, 1.0, 0.0), jnp.where(across < 0, 1.0, 0.0))
+    ):
+        speeds[:, n, :] = value
+    full = width // lanes
+    rest = width - full * lanes
+
+    def turn(tile, carry):
+        u_ref[tile] = x_ref[pl.ds(pl.multiple_of(tile * lanes, lanes), lanes), :].T
+        return carry
+
+    lax.fori_loop(0, full, turn, 0)
+    if rest:
+        u_ref[full] = jnp.zeros_like(u_ref[full])
+        u_ref[full, :, :rest] = x_ref[full * lanes :, :].T
+
+    pl.semaphore_wait(barrier, has_left.astype(jnp.int32) + has_right.astype(jnp.int32) + (parts - 1))
+
+    def to_right(turn, tile):
+        return pltpu.make_async_remote_copy(
+            src_ref=strips.at[turn, tile], dst_ref=from_left.at[turn, tile],
+            send_sem=sent_right.at[turn, tile], recv_sem=got_left.at[turn, tile],
+            device_id={"space": right}, device_id_type=mesh_ids,
+        )
+
+    def to_left(turn, tile):
+        return pltpu.make_async_remote_copy(
+            src_ref=strips.at[turn, tile], dst_ref=from_right.at[turn, tile],
+            send_sem=sent_left.at[turn, tile], recv_sem=got_right.at[turn, tile],
+            device_id={"space": left}, device_id_type=mesh_ids,
+        )
+
+    def send(turn, tile, cells_ref):
+        pack_strips(cells_ref.at[tile], *against_masks(speeds.at[tile]), strips.at[turn, tile])
+
+        @pl.when(has_right)
+        def _():
+            to_right(turn, tile).start()
+
+        @pl.when(has_left)
+        def _():
+            to_left(turn, tile).start()
+
+    def receive(turn, tile):
+        @pl.when(has_left)
+        def _():
+            to_right(turn, tile).wait_recv()
+
+        @pl.when(has_right)
+        def _():
+            to_left(turn, tile).wait_recv()
+
+    def begin(tile, carry):
+        send(0, tile, u_ref)
+        return carry
+
+    lax.fori_loop(0, tiles, begin, 0)
+
+    @pl.when(row == 0)
+    def _():
+        from_left[...] = jnp.zeros_like(from_left)
+
+    @pl.when(row == rows - 1)
+    def _():
+        from_right[...] = jnp.zeros_like(from_right)
+
+    marks = jnp.broadcast_to(mask_ref[...], (GROUP, count)).astype(jnp.float32)
+    before = lax.broadcasted_iota(jnp.int32, (count, count), 0) < lax.broadcasted_iota(jnp.int32, (count, count), 1)
+    rank = dot(marks.astype(jnp.bfloat16), jnp.where(before, 1.0, 0.0).astype(jnp.bfloat16))
+    rank = jnp.where(marks > 0.5, rank, -1.0)[:1].astype(jnp.int32)
+    slot = lax.broadcasted_iota(jnp.int32, (ACT, count), 0)
+    hit = jnp.where(slot == rank, 1.0, 0.0).astype(jnp.bfloat16)
+    pick[:, :count] = hit
+    pick[:, count:] = hit
+    inner = slot % (parts * GROUP)
+    home = (inner // GROUP) * each + (slot // (parts * GROUP)) * GROUP + slot % GROUP
+    hit = jnp.where(home == rank, 1.0, 0.0).T.astype(jnp.bfloat16)
+    spread_back[:, :ACT] = hit
+    spread_back[:, ACT:] = hit
+
+    body = plane // 256 * 256
+    tail = plane - body
+    table[0:body] = plane_ref[0, :body]
+    table[body : 2 * body] = plane_ref[0, :body]
+    table[2 * body : 3 * body] = plane_ref[1, :body]
+    at = 3 * body
+    for part in (0, 0, 1):
+        table[at : at + tail] = plane_ref[part, body:]
+        at += tail
+    if at < table.shape[0]:
+        table[at:] = jnp.zeros_like(table[at:])
+    for i in range(VDIM):
+        columns = slice(i * plane, (i + 1) * plane)
+        first_cube[i] = first_ref[:, columns]
+        second_cube[i] = second_ref[:, columns]
+        loss_cube[i : i + 1] = loss_ref[:, columns]
+
+    def in_copy(tile, n):
+        lane = pl.ds(pl.multiple_of(tile * lanes, lanes), lanes)
+        if n == 0:
+            return pltpu.make_async_copy(sent.at[tile, me], got.at[me, :, lane], own_in.at[tile])
+        return pltpu.make_async_remote_copy(
+            src_ref=sent.at[tile, peers[n]], dst_ref=got.at[me, :, lane],
+            send_sem=sent_in.at[tile, n], recv_sem=got_in.at[tile, n],
+            device_id={"vel": peers[n]}, device_id_type=mesh_ids,
+        )
+
+    def first(tile):
+        receive(0, tile)
+        advance(
+            source, ratio, u_ref.at[tile], None, from_left.at[0, tile], from_right.at[0, tile],
+            speeds.at[tile], one_ref.at[tile], fluxes,
+        )
+        send(1, tile, one_ref)
+
+    def second(tile):
+        receive(1, tile)
+        advance(
+            source, ratio, one_ref.at[tile], u_ref.at[tile], from_left.at[1, tile], from_right.at[1, tile],
+            speeds.at[tile], two_ref.at[tile], fluxes,
+        )
+        high, low = halves(two_ref[tile])
+        sent[tile] = dot(pick[...], jnp.concatenate([high, low], axis=0)).reshape(parts, each, lanes)
+        for n in range(parts):
+            in_copy(tile, n).start()
+
+    def early(tile, carry):
+        first(tile)
+        return carry
+
+    def steady(tile, carry):
+        first(tile)
+        second(tile - LAG)
+        return carry
+
+    def late(tile, carry):
+        second(tile)
+        return carry
+
+    lax.fori_loop(0, LAG, early, 0)
+    lax.fori_loop(LAG, tiles, steady, 0)
+    lax.fori_loop(tiles - LAG, tiles, late, 0)
+
+    def arrive(tile, carry):
+        in_copy(tile, 0).wait()
+        for n in range(1, parts):
+            in_copy(tile, n).wait_recv()
+        return carry
+
+    lax.fori_loop(0, tiles, arrive, 0)
+
+    def write_lhs(at, value):
+        high, low = halves(value)
+        span = slice(at, at + value.shape[0])
+        lhs[span, :body] = high[:, :body]
+        lhs[span, body : 2 * body] = low[:, :body]
+        lhs[span, 2 * body : 3 * body] = high[:, :body]
+        pieces = [high[:, body:], low[:, body:], high[:, body:]]
+        spare = lhs.shape[1] - 3 * plane
+        if spare:
+            pieces.append(jnp.zeros((value.shape[0], spare), jnp.bfloat16))
+        lhs[span, 3 * body :] = jnp.concatenate(pieces, axis=1)
+
+    column_slices = [slice(c, min(c + LANES, plane)) for c in range(0, plane, LANES)]
+
+    def transform(size):
+        mapped[:size] = dot(lhs[:size], table[...])
+
+    def line(columns, step, offset):
+        return dht24(
+            [mapped[i * step + offset : i * step + offset + GROUP, columns] for i in range(VDIM)]
+        )
+
+    def out_copy(chunk, n):
+        if n == 0:
+            return pltpu.make_async_copy(result.at[chunk, me], back.at[chunk, me], own_out.at[chunk])
+        return pltpu.make_async_remote_copy(
+            src_ref=result.at[chunk, peers[n]], dst_ref=back.at[chunk, me],
+            send_sem=sent_out.at[chunk, n], recv_sem=got_out.at[chunk, n],
+            device_id={"vel": peers[n]}, device_id_type=mesh_ids,
+        )
+
+    for chunk in range(chunks):
+        cells = slice(chunk * GROUP, (chunk + 1) * GROUP)
+
+        def cube(i):
+            v, r = divmod(i, planes)
+            return got[v, cells, r * plane : (r + 1) * plane]
+
+        for i in range(0, VDIM, 2):
+            pair = jnp.concatenate([cube(i), cube(i + 1)], axis=0)
+            total[i * GROUP : (i + 2) * GROUP] = -pair
+            write_lhs(i * GROUP, pair)
+        transform(VDIM * GROUP)
+        for columns in column_slices:
+            for i, value in enumerate(line(columns, GROUP, 0)):
+                spectrum[i * GROUP : (i + 1) * GROUP, columns] = value
+        for i in range(0, VDIM, 2):
+            pair = [
+                spectrum[n * GROUP : (n + 1) * GROUP] * loss_cube[n : n + 1] for n in (i, i + 1)
+            ]
+            write_lhs(i * GROUP, jnp.concatenate(pair, axis=0))
+        transform(VDIM * GROUP)
+        for columns in column_slices:
+            for i, value in enumerate(line(columns, GROUP, 0)):
+                at = slice(i * GROUP, (i + 1) * GROUP)
+                total[at, columns] = total[at, columns] * value
+
+        def one(term, carry):
+            for i in range(VDIM):
+                value = spectrum[i * GROUP : (i + 1) * GROUP]
+                pair = [value * cube_ref[i, pl.ds(term, 1), :] for cube_ref in (first_cube, second_cube)]
+                write_lhs(i * 2 * GROUP, jnp.concatenate(pair, axis=0))
+            transform(2 * VDIM * GROUP)
+            for columns in column_slices:
+                image_one = line(columns, 2 * GROUP, 0)
+                image_two = line(columns, 2 * GROUP, GROUP)
+                for i in range(VDIM):
+                    at = slice(i * GROUP, (i + 1) * GROUP)
+                    total[at, columns] += image_one[i] * image_two[i]
+            return carry
+
+        lax.fori_loop(0, terms, one, 0)
+        for i in range(VDIM):
+            v, r = divmod(i, planes)
+            result[chunk, v, :, r * plane : (r + 1) * plane] = total[i * GROUP : (i + 1) * GROUP]
+        for n in range(parts):
+            out_copy(chunk, n).start()
+
+    for chunk in range(chunks):
+        out_copy(chunk, 0).wait()
+        for n in range(1, parts):
+            out_copy(chunk, n).wait_recv()
+
+    def final(tile):
+        lane = pl.ds(pl.multiple_of(tile * lanes, lanes), lanes)
+        high, low = halves(back[:, :, :, lane].reshape(ACT, lanes))
+        change = dot(spread_back[...], jnp.concatenate([high, low], axis=0))
+        return (two_ref[tile] + change).T
+
+    def finish(tile, carry):
+        out_ref[pl.ds(pl.multiple_of(tile * lanes, lanes), lanes), :] = final(tile)
+        return carry
+
+    lax.fori_loop(0, full, finish, 0)
+    if rest:
+        out_ref[full * lanes :, :] = final(full)[:rest]
+
+    def sent_all(tile, carry):
+        for turn in range(2):
+
+            @pl.when(has_right)
+            def _():
+                to_right(turn, tile).wait_send()
+
+            @pl.when(has_left)
+            def _():
+                to_left(turn, tile).wait_send()
+
+        for n in range(1, parts):
+            in_copy(tile, n).wait_send()
+        return carry
+
+    lax.fori_loop(0, tiles, sent_all, 0)
+    for chunk in range(chunks):
+        for n in range(1, parts):
+            out_copy(chunk, n).wait_send()
+
+
+def fused_tables(width):
+    plane = VDIM * VDIM
+    tiles = -(-width // LANES)
+    index = np.arange(tiles * LANES) % width
+    half = (VDIM - 1) / 2.0
+    speed = np.zeros((tiles, 8, LANES), np.float32)
+    speed[:, 0] = (index // plane).reshape(tiles, LANES)
+    second = ((index // VDIM % VDIM).astype(np.float32) - np.float32(half)) / np.float32(half)
+    speed[:, 1] = second.reshape(tiles, LANES)
+    grid = np.arange(VDIM, dtype=np.float64)
+    angle = 2.0 * np.pi * np.outer(grid, grid) / VDIM
+    line = (np.cos(angle) + np.sin(angle)) / np.sqrt(VDIM)
+    wide = (np.kron(line, line) / np.sqrt(VDIM)).astype(np.float32)
+    high = wide.astype(jnp.bfloat16)
+    return speed, np.stack([high, (wide - high.astype(np.float32)).astype(jnp.bfloat16)])
+
+
+def fused(distribution, neighbours, block_level, collide_mask, gain_first, gain_second, loss_rates):
+    _, count, width = distribution.shape
+    parts = lax.axis_size("vel")
+    plane = VDIM * VDIM
+    tiles = pl.cdiv(width, LANES)
+    wide = tiles * LANES
+    each = ACT // parts
+    chunks = each // GROUP
+    terms = gain_first.shape[0]
+    depth = pl.cdiv(3 * plane, 256) * 256
+    smem = pl.BlockSpec(memory_space=pltpu.SMEM)
+    vmem = pl.BlockSpec(memory_space=pltpu.VMEM)
+    speed, planes = fused_tables(width)
+    f32, bf16 = jnp.float32, jnp.bfloat16
+    strips = pltpu.VMEM((2, tiles, 10 * BSIDE, LANES), f32)
+    dma = pltpu.SemaphoreType.DMA
+    return pl.pallas_call(
+        fused_kernel,
+        in_specs=[smem, smem] + [vmem] * 7,
+        out_specs=vmem,
+        out_shape=jax.ShapeDtypeStruct((width, count), f32),
+        scratch_shapes=[pltpu.VMEM((tiles, count, LANES), f32)] * 3
+        + [pltpu.VMEM((count, LANES), f32)] * 3
+        + [pltpu.VMEM((tiles, 8, LANES), f32)]
+        + [strips] * 3
+        + [pltpu.VMEM((ACT, 2 * count), bf16), pltpu.VMEM((count, 2 * ACT), bf16)]
+        + [pltpu.VMEM((depth, plane), bf16)]
+        + [pltpu.VMEM((VDIM, terms, plane), f32)] * 2
+        + [pltpu.VMEM((VDIM, plane), f32)]
+        + [pltpu.VMEM((2 * VDIM * GROUP, depth), bf16), pltpu.VMEM((2 * VDIM * GROUP, plane), f32)]
+        + [pltpu.VMEM((VDIM * GROUP, plane), f32)] * 2
+        + [pltpu.VMEM((tiles, parts, each, LANES), f32), pltpu.VMEM((parts, each, wide), f32)]
+        + [pltpu.VMEM((chunks, parts, GROUP, wide), f32)] * 2
+        + [dma((2, tiles))] * 4
+        + [dma((tiles, parts)), dma((tiles, parts)), dma((tiles,))]
+        + [dma((chunks, parts)), dma((chunks, parts)), dma((chunks,))],
+        compiler_params=pltpu.CompilerParams(
+            collective_id=2, has_side_effects=True, vmem_limit_bytes=60 * 1024 * 1024
+        ),
+    )(
+        neighbours[0], block_level, distribution.reshape(count, width).T, collide_mask[None],
+        gain_first, gain_second, loss_rates[None], jnp.asarray(planes), jnp.asarray(speed),
+    )
+
+
 def shards(
     distribution, neighbours, block_level, collide_mask, gain_first, gain_second, loss_rates
 ):
     blocks, cell_count, width = distribution.shape
     assert blocks == 1
+    parts = lax.axis_size("vel")
+    plane = VDIM * VDIM
+    if width % plane == 0 and ACT % (parts * GROUP) == 0:
+        cells = fused(
+            distribution, neighbours, block_level, collide_mask, gain_first, gain_second, loss_rates
+        )
+        return cells.T.reshape(blocks, cell_count, width)
     density = distribution.reshape(cell_count, width)
     speeds = speed_rows(lax.axis_index("vel") * width, width)
     ratio = courant * jnp.exp2(block_level.astype(jnp.float32))

time: 108 us -> 88.7 us (0.82); the launches traced: 106 us -> 88.5 us
  Pallas kernels: 89.8 us -> 83.6 us
  local copies, waits for them, and re-layouts: 10.2 us -> 4.28 us
  other arithmetic: 5.2 us -> 0 us
    pallas_call x4 -> x1, Pallas kernels: 89.8 us -> 83.6 us  [fused(): pl.pallas_call(fused_kernel, in_specs=[smem, smem] + [vmem] * 7, out_spec...]
    reshape x2 -> x0, local copies, waits for them, and re-layouts: 4.5 us -> none  [the longest x1 2.7 us: shards(): scatter(chosen, held, section_two, change)]
    reduce_sum x3 -> x0, other arithmetic: 2.87 us -> none  [the longest x1 1.34 us: shards(): held = jnp.sum(collide_mask)[None]]
    pad x1 -> x0, local copies, waits for them, and re-layouts: 2.85 us -> none  [tiled(): rows = jnp.pad(rows, ((0, 0), (0, tiles * LANES - width)))]
    unnamed x2 -> x1, local copies, waits for them, and re-layouts: 1.25 us -> 2.8 us
where the time goes in v1:
time: 88.7 us; the launch traced here: 88.5 us
  Pallas kernels  83.6 us (94%)
  local copies, waits for them, and re-layouts  4.28 us (5%)
    pallas_call x1, Pallas kernels, fused(): pl.pallas_call(fused_kernel, in_specs=[smem, smem] + [vmem] * 7, out_spec...  83.6 us
    unnamed x1, local copies, waits for them, and re-layouts  2.8 us

profile of v1, /device:TPU:1, one launch (start us, length us, event | category | flops | bytes accessed | tf_op | source)
XLA Modules:
  0.0 88.5 jit_solution(4332367304542343147)
XLA Ops:
  0.7 1.5 %broadcast_in_dim.7.loss_ref = f32[1,13824]{1,0:T(1,128)} reshape(f32[13824]{0:T(1024)} %param.15) | data formatting | bytes 110592 | tf_op jit(solution)/shard_map/broadcast_in_dim | solution.py:922
  2.1 83.6 %shard_map.91 = f32[1728,256]{1,0:T(8,128)} custom-call(s32[4]{0:T(128)} %bitcast.11, s32[1]{0:T(128)S(6)} %copy.11.level_ref, f32[1728,256]{1,0:T(8,128)} %bitcast.9, s32[1,256]{1,0:T(1,128)} %bitcast.10, f32[6,13824]{1,0:T(8,128)} %first_ref.1, f32[6,13824]{1,0:T(8,128)} %second_ref.1, f32[1,13824]{1,0:T(1,128)} %broadcast_in_dim.7.loss_ref, ...), custom_call_target="tpu_custom_call" | custom-call | tf_op jit(solution)/shard_map/pallas_call | solution.py:897
  85.7 2.8 %copy.12 = f32[1,256,1728]{1,2,0:T(8,128)} copy(f32[1,256,1728]{1,2,0:T(8,128)} %bitcast.8) | data formatting | bytes 3538944

commit v2 on v1

--- a/solution.py
+++ b/solution.py
@@ -543,17 +543,20 @@
 
 
 LAG = 2
+AHEAD = 3
 
 
 def fused_kernel(
-    near_ref, level_ref, x_ref, mask_ref, first_ref, second_ref, loss_ref, plane_ref, speed_ref, out_ref,
+    near_hbm, level_hbm, x_hbm, mask_hbm, first_hbm, second_hbm, loss_hbm, plane_hbm, speed_hbm, out_ref,
+    near_ref, level_ref, x_ref, mask_ref, first_ref, second_ref, loss_ref, plane_ref, speed_ref,
     u_ref, one_ref, two_ref, flux_one, flux_two, flux_turned, speeds, strips, from_left, from_right,
     pick, spread_back, table, first_cube, second_cube, loss_cube, lhs, mapped, spectrum, total,
     sent, got, result, back,
     sent_left, sent_right, got_left, got_right, sent_in, got_in, own_in, sent_out, got_out, own_out,
+    x_here, here,
 ):
     tiles, count, lanes = u_ref.shape
-    width = x_ref.shape[0]
+    width = x_hbm.shape[0]
     parts, each, wide = got.shape
     chunks = result.shape[0]
     plane = VDIM * VDIM
@@ -568,6 +571,26 @@
     mesh_ids = pl.DeviceIdType.MESH
     fluxes = (flux_one, flux_two, flux_turned)
 
+    early_rows = AHEAD * lanes
+    cells_here = [
+        pltpu.make_async_copy(x_hbm.at[:early_rows], x_ref.at[:early_rows], x_here.at[0]),
+        pltpu.make_async_copy(x_hbm.at[early_rows:], x_ref.at[early_rows:width], x_here.at[1]),
+    ]
+    near_here, level_here, mask_here, first_here, second_here, loss_here, plane_here, speed_here = [
+        pltpu.make_async_copy(source, target, here.at[n])
+        for n, (source, target) in enumerate(
+            (
+                (near_hbm, near_ref), (level_hbm, level_ref), (mask_hbm, mask_ref), (first_hbm, first_ref),
+                (second_hbm, second_ref), (loss_hbm, loss_ref), (plane_hbm, plane_ref), (speed_hbm, speed_ref),
+            )
+        )
+    ]
+    speed_here.start()
+    for copy in cells_here:
+        copy.start()
+    for copy in (near_here, level_here, mask_here, plane_here, first_here, second_here, loss_here):
+        copy.start()
+
     barrier = pltpu.get_barrier_semaphore()
 
     @pl.when(has_left)
@@ -581,13 +604,7 @@
     for peer in peers[1:]:
         pl.semaphore_signal(barrier, inc=1, device_id={"vel": peer}, device_id_type=mesh_ids)
 
-    ratio = courant * jnp.left_shift(1, level_ref[0]).astype(jnp.float32)
-    source = []
-    for face in range(4):
-        for step in (-1, 0, 1):
-            held = (near_ref[face] == row + step) & (near_ref[face] >= 0)
-            source.append(jnp.where(held, 1.0, 0.0))
-
+    speed_here.wait()
     half = (VDIM - 1) / 2.0
     start = (me * planes).astype(jnp.float32)
     toward = (speed_ref[:, 0, :] + start - half) / half
@@ -599,14 +616,7 @@
     full = width // lanes
     rest = width - full * lanes
 
-    def turn(tile, carry):
-        u_ref[tile] = x_ref[pl.ds(pl.multiple_of(tile * lanes, lanes), lanes), :].T
-        return carry
-
-    lax.fori_loop(0, full, turn, 0)
-    if rest:
-        u_ref[full] = jnp.zeros_like(u_ref[full])
-        u_ref[full, :, :rest] = x_ref[full * lanes :, :].T
+    x_ref[width:] = jnp.zeros_like(x_ref[width:])
 
     pl.semaphore_wait(barrier, has_left.astype(jnp.int32) + has_right.astype(jnp.int32) + (parts - 1))
 
@@ -644,11 +654,16 @@
         def _():
             to_left(turn, tile).wait_recv()
 
+    def launch(tile):
+        u_ref[tile] = x_ref[pl.ds(pl.multiple_of(tile * lanes, lanes), lanes), :].T
+        send(0, tile, u_ref)
+
     def begin(tile, carry):
-        send(0, tile, u_ref)
-        return carry
-
-    lax.fori_loop(0, tiles, begin, 0)
+        launch(tile)
+        return carry
+
+    cells_here[0].wait()
+    lax.fori_loop(0, AHEAD, begin, 0)
 
     @pl.when(row == 0)
     def _():
@@ -658,6 +673,15 @@
     def _():
         from_right[...] = jnp.zeros_like(from_right)
 
+    near_here.wait()
+    level_here.wait()
+    ratio = courant * jnp.left_shift(1, level_ref[0]).astype(jnp.float32)
+    source = []
+    for face in range(4):
+        for step in (-1, 0, 1):
+            held = (near_ref[0, face] == row + step) & (near_ref[0, face] >= 0)
+            source.append(jnp.where(held, 1.0, 0.0))
+    mask_here.wait()
     marks = jnp.broadcast_to(mask_ref[...], (GROUP, count)).astype(jnp.float32)
     before = lax.broadcasted_iota(jnp.int32, (count, count), 0) < lax.broadcasted_iota(jnp.int32, (count, count), 1)
     rank = dot(marks.astype(jnp.bfloat16), jnp.where(before, 1.0, 0.0).astype(jnp.bfloat16))
@@ -666,12 +690,15 @@
     hit = jnp.where(slot == rank, 1.0, 0.0).astype(jnp.bfloat16)
     pick[:, :count] = hit
     pick[:, count:] = hit
-    inner = slot % (parts * GROUP)
-    home = (inner // GROUP) * each + (slot // (parts * GROUP)) * GROUP + slot % GROUP
-    hit = jnp.where(home == rank, 1.0, 0.0).T.astype(jnp.bfloat16)
-    spread_back[:, :ACT] = hit
-    spread_back[:, ACT:] = hit
-
+    slot = lax.broadcasted_iota(jnp.int32, (parts * GROUP, count), 0)
+    for chunk in range(chunks):
+        home = (slot // GROUP) * each + chunk * GROUP + slot % GROUP
+        hit = jnp.where(home == rank, 1.0, 0.0).astype(jnp.bfloat16)
+        spread_back[chunk, : parts * GROUP] = hit
+        spread_back[chunk, parts * GROUP :] = hit
+
+    for copy in (plane_here, first_here, second_here, loss_here, cells_here[1]):
+        copy.wait()
     body = plane // 256 * 256
     tail = plane - body
     table[0:body] = plane_ref[0, :body]
@@ -687,10 +714,15 @@
         columns = slice(i * plane, (i + 1) * plane)
         first_cube[i] = first_ref[:, columns]
         second_cube[i] = second_ref[:, columns]
-        loss_cube[i : i + 1] = loss_ref[:, columns]
+        done = 0
+        while done < plane:
+            line_at, lane_at = divmod(i * plane + done, lanes)
+            span = min(lanes - lane_at, plane - done)
+            loss_cube[i : i + 1, done : done + span] = loss_ref[line_at : line_at + 1, lane_at : lane_at + span]
+            done += span
 
     def in_copy(tile, n):
-        lane = pl.ds(pl.multiple_of(tile * lanes, lanes), lanes)
+        lane = pl.ds(pl.multiple_of(tile * 2 * lanes, 2 * lanes), 2 * lanes)
         if n == 0:
             return pltpu.make_async_copy(sent.at[tile, me], got.at[me, :, lane], own_in.at[tile])
         return pltpu.make_async_remote_copy(
@@ -714,15 +746,25 @@
             speeds.at[tile], two_ref.at[tile], fluxes,
         )
         high, low = halves(two_ref[tile])
-        sent[tile] = dot(pick[...], jnp.concatenate([high, low], axis=0)).reshape(parts, each, lanes)
-        for n in range(parts):
-            in_copy(tile, n).start()
+        picked = dot(pick[...], jnp.concatenate([high, low], axis=0)).reshape(parts, each, lanes)
+        side = lax.rem(tile, 2)
+        sent[tile // 2, :, :, pl.ds(pl.multiple_of(side * lanes, lanes), lanes)] = picked
+
+        @pl.when(side == 1)
+        def _():
+            for n in range(parts):
+                in_copy(tile // 2, n).start()
 
     def early(tile, carry):
+        launch(tile + AHEAD)
         first(tile)
         return carry
 
     def steady(tile, carry):
+        @pl.when(tile + AHEAD < tiles)
+        def _():
+            launch(tile + AHEAD)
+
         first(tile)
         second(tile - LAG)
         return carry
@@ -741,7 +783,7 @@
             in_copy(tile, n).wait_recv()
         return carry
 
-    lax.fori_loop(0, tiles, arrive, 0)
+    lax.fori_loop(0, tiles // 2, arrive, 0)
 
     def write_lhs(at, value):
         high, low = halves(value)
@@ -821,49 +863,66 @@
         for n in range(parts):
             out_copy(chunk, n).start()
 
+    def sent_all(tile, carry):
+        for turn in range(2):
+
+            @pl.when(has_right)
+            def _():
+                to_right(turn, tile).wait_send()
+
+            @pl.when(has_left)
+            def _():
+                to_left(turn, tile).wait_send()
+
+        return carry
+
+    lax.fori_loop(0, tiles, sent_all, 0)
+
+    def inward_sent(pair, carry):
+        for n in range(1, parts):
+            in_copy(pair, n).wait_send()
+        return carry
+
+    lax.fori_loop(0, tiles // 2, inward_sent, 0)
+
+    held = parts * GROUP
     for chunk in range(chunks):
+        last = chunk == chunks - 1
         out_copy(chunk, 0).wait()
         for n in range(1, parts):
             out_copy(chunk, n).wait_recv()
 
-    def final(tile):
-        lane = pl.ds(pl.multiple_of(tile * lanes, lanes), lanes)
-        high, low = halves(back[:, :, :, lane].reshape(ACT, lanes))
-        change = dot(spread_back[...], jnp.concatenate([high, low], axis=0))
-        return (two_ref[tile] + change).T
-
-    def finish(tile, carry):
-        out_ref[pl.ds(pl.multiple_of(tile * lanes, lanes), lanes), :] = final(tile)
-        return carry
-
-    lax.fori_loop(0, full, finish, 0)
-    if rest:
-        out_ref[full * lanes :, :] = final(full)[:rest]
-
-    def sent_all(tile, carry):
-        for turn in range(2):
-
-            @pl.when(has_right)
-            def _():
-                to_right(turn, tile).wait_send()
-
-            @pl.when(has_left)
-            def _():
-                to_left(turn, tile).wait_send()
-
-        for n in range(1, parts):
-            in_copy(tile, n).wait_send()
-        return carry
-
-    lax.fori_loop(0, tiles, sent_all, 0)
-    for chunk in range(chunks):
+        def change(tile):
+            at = tile * lanes if last else pl.multiple_of(tile * lanes, lanes)
+            turned = back[chunk, :, :, pl.ds(at, lanes)].reshape(held, lanes).T
+            high, low = halves(turned)
+            return dot(jnp.concatenate([high, low], axis=1), spread_back[chunk])
+
+        def settle(tile, carry):
+            at = pl.ds(pl.multiple_of(tile * lanes, lanes), lanes)
+            if chunk == 0:
+                out_ref[at, :] = two_ref[tile].T + change(tile)
+            else:
+                out_ref[at, :] += change(tile)
+            return carry
+
+        if last and chunk > 0:
+            for tile in range(full):
+                out_ref[tile * lanes : (tile + 1) * lanes, :] += change(tile)
+        else:
+            lax.fori_loop(0, full, settle, 0)
+        if rest:
+            if chunk == 0:
+                out_ref[full * lanes :, :] = (two_ref[full].T + change(full))[:rest]
+            else:
+                out_ref[full * lanes :, :] += change(full)[:rest]
         for n in range(1, parts):
             out_copy(chunk, n).wait_send()
 
 
 def fused_tables(width):
     plane = VDIM * VDIM
-    tiles = -(-width // LANES)
+    tiles = 2 * -(-width // (2 * LANES))
     index = np.arange(tiles * LANES) % width
     half = (VDIM - 1) / 2.0
     speed = np.zeros((tiles, 8, LANES), np.float32)
@@ -882,44 +941,47 @@
     _, count, width = distribution.shape
     parts = lax.axis_size("vel")
     plane = VDIM * VDIM
-    tiles = pl.cdiv(width, LANES)
+    tiles = 2 * pl.cdiv(width, 2 * LANES)
     wide = tiles * LANES
     each = ACT // parts
     chunks = each // GROUP
     terms = gain_first.shape[0]
     depth = pl.cdiv(3 * plane, 256) * 256
-    smem = pl.BlockSpec(memory_space=pltpu.SMEM)
-    vmem = pl.BlockSpec(memory_space=pltpu.VMEM)
+    smem, f32, bf16 = pltpu.SMEM, jnp.float32, jnp.bfloat16
     speed, planes = fused_tables(width)
-    f32, bf16 = jnp.float32, jnp.bfloat16
     strips = pltpu.VMEM((2, tiles, 10 * BSIDE, LANES), f32)
     dma = pltpu.SemaphoreType.DMA
     return pl.pallas_call(
         fused_kernel,
-        in_specs=[smem, smem] + [vmem] * 7,
-        out_specs=vmem,
-        out_shape=jax.ShapeDtypeStruct((width, count), f32),
-        scratch_shapes=[pltpu.VMEM((tiles, count, LANES), f32)] * 3
+        in_specs=[pl.BlockSpec(memory_space=pltpu.HBM)] * 9,
+        out_specs=pl.BlockSpec(memory_space=pltpu.VMEM),
+        out_shape=pltpu.VMEM((width, count), f32),
+        scratch_shapes=[smem((1, 4), jnp.int32), smem((1,), jnp.int32), pltpu.VMEM((wide, count), f32)]
+        + [pltpu.VMEM((1, count), jnp.int32)]
+        + [pltpu.VMEM(gain_first.shape, f32)] * 2
+        + [pltpu.VMEM((loss_rates.size // LANES, LANES), f32)]
+        + [pltpu.VMEM(planes.shape, bf16), pltpu.VMEM(speed.shape, f32)]
+        + [pltpu.VMEM((tiles, count, LANES), f32)] * 3
         + [pltpu.VMEM((count, LANES), f32)] * 3
         + [pltpu.VMEM((tiles, 8, LANES), f32)]
         + [strips] * 3
-        + [pltpu.VMEM((ACT, 2 * count), bf16), pltpu.VMEM((count, 2 * ACT), bf16)]
+        + [pltpu.VMEM((ACT, 2 * count), bf16), pltpu.VMEM((chunks, 2 * parts * GROUP, count), bf16)]
         + [pltpu.VMEM((depth, plane), bf16)]
         + [pltpu.VMEM((VDIM, terms, plane), f32)] * 2
         + [pltpu.VMEM((VDIM, plane), f32)]
         + [pltpu.VMEM((2 * VDIM * GROUP, depth), bf16), pltpu.VMEM((2 * VDIM * GROUP, plane), f32)]
         + [pltpu.VMEM((VDIM * GROUP, plane), f32)] * 2
-        + [pltpu.VMEM((tiles, parts, each, LANES), f32), pltpu.VMEM((parts, each, wide), f32)]
+        + [pltpu.VMEM((tiles // 2, parts, each, 2 * LANES), f32), pltpu.VMEM((parts, each, wide), f32)]
         + [pltpu.VMEM((chunks, parts, GROUP, wide), f32)] * 2
         + [dma((2, tiles))] * 4
-        + [dma((tiles, parts)), dma((tiles, parts)), dma((tiles,))]
-        + [dma((chunks, parts)), dma((chunks, parts)), dma((chunks,))],
+        + [dma((tiles // 2, parts)), dma((tiles // 2, parts)), dma((tiles // 2,))]
+        + [dma((chunks, parts)), dma((chunks, parts)), dma((chunks,)), dma((2,)), dma((8,))],
         compiler_params=pltpu.CompilerParams(
-            collective_id=2, has_side_effects=True, vmem_limit_bytes=60 * 1024 * 1024
+            collective_id=2, has_side_effects=True, vmem_limit_bytes=56 * 1024 * 1024
         ),
     )(
-        neighbours[0], block_level, distribution.reshape(count, width).T, collide_mask[None],
-        gain_first, gain_second, loss_rates[None], jnp.asarray(planes), jnp.asarray(speed),
+        neighbours, block_level, distribution.reshape(count, width).T, collide_mask[None],
+        gain_first, gain_second, loss_rates.reshape(-1, LANES), jnp.asarray(planes), jnp.asarray(speed),
     )
 
 

time: 88.7 us -> 73.6 us (0.83)
  Pallas kernels: 83.6 us -> 71.3 us
  local copies, waits for them, and re-layouts: 4.28 us -> 1.21 us
    pallas_call x1, Pallas kernels: 83.6 us -> 71.3 us  [fused(): pl.pallas_call(fused_kernel, in_specs=[pl.BlockSpec(memory_space=pltpu.HB...]
    unnamed x1, local copies, waits for them, and re-layouts: 2.8 us -> 1.21 us
    broadcast_in_dim x1 -> x0, local copies, waits for them, and re-layouts: 1.48 us -> none  [fused(): loss_rates[None]]
where the time goes in v2:
time: 73.6 us; the launch traced here: 73.2 us
  Pallas kernels  71.3 us (97%)
  local copies, waits for them, and re-layouts  1.21 us (2%)
    pallas_call x1, Pallas kernels, fused(): pl.pallas_call(fused_kernel, in_specs=[pl.BlockSpec(memory_space=pltpu.HB...  71.3 us

profile of v2, /device:TPU:1, one launch (start us, length us, event | category | flops | bytes accessed | tf_op | source)
XLA Modules:
  0.0 73.2 jit_solution(1491113114749117713)
XLA Ops:
  0.7 71.3 %shard_map.91 = f32[1728,256]{1,0:T(8,128)S(1)} custom-call(s32[1,4]{1,0:T(1,128)} %near_hbm.1, s32[1]{0:T(128)S(6)} %copy.12.level_hbm, f32[1728,256]{1,0:T(8,128)} %bitcast.9, s32[1,256]{1,0:T(1,128)} %bitcast.11, f32[6,13824]{1,0:T(8,128)} %first_hbm.1, f32[6,13824]{1,0:T(8,128)} %second_hbm.1, f32[108,128]{1,0:T(8,128)} %bitcast.10, ...), custom_call_target="tpu_custom_call" | custom-call | tf_op jit(solution)/shard_map/pallas_call | solution.py:954
  71.9 1.2 %copy.11 = f32[1,256,1728]{1,2,0:T(8,128)} copy(f32[1,256,1728]{1,2,0:T(8,128)S(1)} %bitcast.8) | data formatting | bytes 3538944

commit v3 on v2

--- a/solution.py
+++ b/solution.py
@@ -542,6 +542,7 @@
     return result
 
 
+HALF = GROUP // 2
 LAG = 2
 AHEAD = 3
 
@@ -549,8 +550,8 @@
 def fused_kernel(
     near_hbm, level_hbm, x_hbm, mask_hbm, first_hbm, second_hbm, loss_hbm, plane_hbm, speed_hbm, out_ref,
     near_ref, level_ref, x_ref, mask_ref, first_ref, second_ref, loss_ref, plane_ref, speed_ref,
-    u_ref, one_ref, two_ref, flux_one, flux_two, flux_turned, speeds, strips, from_left, from_right,
-    pick, spread_back, table, first_cube, second_cube, loss_cube, lhs, mapped, spectrum, total,
+    u_ref, one_ref, two_ref, turned, flux_one, flux_two, flux_turned, speeds, strips, from_left, from_right,
+    pick, spread_back, table, first_cube, second_cube, gains, loss_cube, lhs, mapped, spectrum, doubled, loss, total, flat,
     sent, got, result, back,
     sent_left, sent_right, got_left, got_right, sent_in, got_in, own_in, sent_out, got_out, own_out,
     x_here, here,
@@ -613,9 +614,6 @@
         (jnp.abs(toward), jnp.abs(across), jnp.where(toward < 0, 1.0, 0.0), jnp.where(across < 0, 1.0, 0.0))
     ):
         speeds[:, n, :] = value
-    full = width // lanes
-    rest = width - full * lanes
-
     x_ref[width:] = jnp.zeros_like(x_ref[width:])
 
     pl.semaphore_wait(barrier, has_left.astype(jnp.int32) + has_right.astype(jnp.int32) + (parts - 1))
@@ -690,12 +688,15 @@
     hit = jnp.where(slot == rank, 1.0, 0.0).astype(jnp.bfloat16)
     pick[:, :count] = hit
     pick[:, count:] = hit
-    slot = lax.broadcasted_iota(jnp.int32, (parts * GROUP, count), 0)
+    held = parts * GROUP
+    slot = lax.broadcasted_iota(jnp.int32, (held, count), 0)
     for chunk in range(chunks):
-        home = (slot // GROUP) * each + chunk * GROUP + slot % GROUP
-        hit = jnp.where(home == rank, 1.0, 0.0).astype(jnp.bfloat16)
-        spread_back[chunk, : parts * GROUP] = hit
-        spread_back[chunk, parts * GROUP :] = hit
+        home = (slot // GROUP) * each + chunk * HALF + slot % HALF
+        for side in range(2):
+            own = (home == rank) & (slot % GROUP // HALF == side)
+            hit = jnp.where(own, 1.0, 0.0).astype(jnp.bfloat16)
+            for at in (chunk % 2 * held, (2 + chunk % 2) * held):
+                spread_back[chunk // 2, side, at : at + held] = hit
 
     for copy in (plane_here, first_here, second_here, loss_here, cells_here[1]):
         copy.wait()
@@ -721,13 +722,27 @@
             loss_cube[i : i + 1, done : done + span] = loss_ref[line_at : line_at + 1, lane_at : lane_at + span]
             done += span
 
+    upper = lax.broadcasted_iota(jnp.int32, (GROUP, plane), 0) < HALF
+
+    def lay(i, carry):
+        for term in range(terms):
+            one_row = jnp.broadcast_to(first_cube[i, term : term + 1, :], (GROUP, plane))
+            two_row = jnp.broadcast_to(second_cube[i, term : term + 1, :], (GROUP, plane))
+            gains[term, i] = jnp.where(upper, one_row, two_row)
+        return carry
+
+    lax.fori_loop(0, VDIM, lay, 0)
+
+    def all_of(ref, sem):
+        pltpu.make_async_copy(ref, ref, sem).wait()
+
     def in_copy(tile, n):
         lane = pl.ds(pl.multiple_of(tile * 2 * lanes, 2 * lanes), 2 * lanes)
         if n == 0:
             return pltpu.make_async_copy(sent.at[tile, me], got.at[me, :, lane], own_in.at[tile])
         return pltpu.make_async_remote_copy(
             src_ref=sent.at[tile, peers[n]], dst_ref=got.at[me, :, lane],
-            send_sem=sent_in.at[tile, n], recv_sem=got_in.at[tile, n],
+            send_sem=sent_in.at[tile], recv_sem=got_in.at[tile],
             device_id={"vel": peers[n]}, device_id_type=mesh_ids,
         )
 
@@ -743,9 +758,10 @@
         receive(1, tile)
         advance(
             source, ratio, one_ref.at[tile], u_ref.at[tile], from_left.at[1, tile], from_right.at[1, tile],
-            speeds.at[tile], two_ref.at[tile], fluxes,
-        )
-        high, low = halves(two_ref[tile])
+            speeds.at[tile], two_ref, fluxes,
+        )
+        turned[tile] = two_ref[...].T
+        high, low = halves(two_ref[...])
         picked = dot(pick[...], jnp.concatenate([high, low], axis=0)).reshape(parts, each, lanes)
         side = lax.rem(tile, 2)
         sent[tile // 2, :, :, pl.ds(pl.multiple_of(side * lanes, lanes), lanes)] = picked
@@ -779,8 +795,7 @@
 
     def arrive(tile, carry):
         in_copy(tile, 0).wait()
-        for n in range(1, parts):
-            in_copy(tile, n).wait_recv()
+        all_of(got.at[1:, :, pl.ds(pl.multiple_of(tile * 2 * lanes, 2 * lanes), 2 * lanes)], got_in.at[tile])
         return carry
 
     lax.fori_loop(0, tiles // 2, arrive, 0)
@@ -802,22 +817,26 @@
     def transform(size):
         mapped[:size] = dot(lhs[:size], table[...])
 
-    def line(columns, step, offset):
-        return dht24(
-            [mapped[i * step + offset : i * step + offset + GROUP, columns] for i in range(VDIM)]
-        )
+    def line(columns, many=1, n=0):
+        starts = [(i * many + n) * GROUP for i in range(VDIM)]
+        return dht24([mapped[at : at + GROUP, columns] for at in starts])
 
     def out_copy(chunk, n):
         if n == 0:
             return pltpu.make_async_copy(result.at[chunk, me], back.at[chunk, me], own_out.at[chunk])
         return pltpu.make_async_remote_copy(
             src_ref=result.at[chunk, peers[n]], dst_ref=back.at[chunk, me],
-            send_sem=sent_out.at[chunk, n], recv_sem=got_out.at[chunk, n],
+            send_sem=sent_out.at[chunk], recv_sem=got_out.at[chunk],
             device_id={"vel": peers[n]}, device_id_type=mesh_ids,
         )
 
-    for chunk in range(chunks):
-        cells = slice(chunk * GROUP, (chunk + 1) * GROUP)
+    def double(value, half):
+        other = pltpu.roll(value, HALF, 0)
+        return jnp.where(upper, value, other) if half == 0 else jnp.where(upper, other, value)
+
+    part = wide // 2
+    for group in range(chunks // 2):
+        cells = slice(group * GROUP, (group + 1) * GROUP)
 
         def cube(i):
             v, r = divmod(i, planes)
@@ -825,11 +844,11 @@
 
         for i in range(0, VDIM, 2):
             pair = jnp.concatenate([cube(i), cube(i + 1)], axis=0)
-            total[i * GROUP : (i + 2) * GROUP] = -pair
+            loss[i * GROUP : (i + 2) * GROUP] = -pair
             write_lhs(i * GROUP, pair)
         transform(VDIM * GROUP)
         for columns in column_slices:
-            for i, value in enumerate(line(columns, GROUP, 0)):
+            for i, value in enumerate(line(columns)):
                 spectrum[i * GROUP : (i + 1) * GROUP, columns] = value
         for i in range(0, VDIM, 2):
             pair = [
@@ -838,30 +857,43 @@
             write_lhs(i * GROUP, jnp.concatenate(pair, axis=0))
         transform(VDIM * GROUP)
         for columns in column_slices:
-            for i, value in enumerate(line(columns, GROUP, 0)):
+            for i, value in enumerate(line(columns)):
                 at = slice(i * GROUP, (i + 1) * GROUP)
-                total[at, columns] = total[at, columns] * value
-
-        def one(term, carry):
+                loss[at, columns] = loss[at, columns] * value
+
+        for half in range(2):
+            chunk = 2 * group + half
             for i in range(VDIM):
-                value = spectrum[i * GROUP : (i + 1) * GROUP]
-                pair = [value * cube_ref[i, pl.ds(term, 1), :] for cube_ref in (first_cube, second_cube)]
-                write_lhs(i * 2 * GROUP, jnp.concatenate(pair, axis=0))
-            transform(2 * VDIM * GROUP)
-            for columns in column_slices:
-                image_one = line(columns, 2 * GROUP, 0)
-                image_two = line(columns, 2 * GROUP, GROUP)
+                at = slice(i * GROUP, (i + 1) * GROUP)
+                doubled[at] = double(spectrum[at], half)
+                total[at] = double(loss[at], half)
+
+            def some(step, carry):
                 for i in range(VDIM):
-                    at = slice(i * GROUP, (i + 1) * GROUP)
-                    total[at, columns] += image_one[i] * image_two[i]
-            return carry
-
-        lax.fori_loop(0, terms, one, 0)
-        for i in range(VDIM):
-            v, r = divmod(i, planes)
-            result[chunk, v, :, r * plane : (r + 1) * plane] = total[i * GROUP : (i + 1) * GROUP]
-        for n in range(parts):
-            out_copy(chunk, n).start()
+                    value = doubled[i * GROUP : (i + 1) * GROUP]
+                    pair = [value * gains[2 * step + n, i] for n in range(2)]
+                    write_lhs(i * 2 * GROUP, jnp.concatenate(pair, axis=0))
+                transform(2 * VDIM * GROUP)
+                for columns in column_slices:
+                    images = [line(columns, 2, n) for n in range(2)]
+                    for i in range(VDIM):
+                        at = slice(i * GROUP, (i + 1) * GROUP)
+                        both = [image[i] * pltpu.roll(image[i], HALF, 0) for image in images]
+                        total[at, columns] += both[0] + both[1]
+                return carry
+
+            lax.fori_loop(0, terms // 2, some, 0)
+            low_rows = upper[:, :LANES]
+            for v in range(parts):
+                for r in range(planes):
+                    i = v * planes + r
+                    flat[v, :, r * plane : (r + 1) * plane] = total[i * GROUP : (i + 1) * GROUP]
+                for at in range(0, part, LANES):
+                    result[chunk, v, :, at : at + LANES] = jnp.where(
+                        low_rows, flat[v, :, at : at + LANES], flat[v, :, part + at : part + at + LANES]
+                    )
+            for n in range(parts):
+                out_copy(chunk, n).start()
 
     def sent_all(tile, carry):
         for turn in range(2):
@@ -879,45 +911,44 @@
     lax.fori_loop(0, tiles, sent_all, 0)
 
     def inward_sent(pair, carry):
-        for n in range(1, parts):
-            in_copy(pair, n).wait_send()
+        all_of(sent.at[pair, 1:], sent_in.at[pair])
         return carry
 
     lax.fori_loop(0, tiles // 2, inward_sent, 0)
 
-    held = parts * GROUP
-    for chunk in range(chunks):
-        last = chunk == chunks - 1
-        out_copy(chunk, 0).wait()
-        for n in range(1, parts):
-            out_copy(chunk, n).wait_recv()
-
-        def change(tile):
-            at = tile * lanes if last else pl.multiple_of(tile * lanes, lanes)
-            turned = back[chunk, :, :, pl.ds(at, lanes)].reshape(held, lanes).T
-            high, low = halves(turned)
-            return dot(jnp.concatenate([high, low], axis=1), spread_back[chunk])
-
-        def settle(tile, carry):
-            at = pl.ds(pl.multiple_of(tile * lanes, lanes), lanes)
-            if chunk == 0:
-                out_ref[at, :] = two_ref[tile].T + change(tile)
-            else:
-                out_ref[at, :] += change(tile)
-            return carry
-
-        if last and chunk > 0:
-            for tile in range(full):
-                out_ref[tile * lanes : (tile + 1) * lanes, :] += change(tile)
+    half_tiles = tiles // 2
+    for chunk in range(chunks - 1):
+        all_of(result.at[chunk, 1:], sent_out.at[chunk])
+
+    def change(pair, side, column):
+        blocks = [
+            back[chunk, :, :, pl.ds(column, lanes)].reshape(held, lanes) for chunk in (2 * pair, 2 * pair + 1)
+        ]
+        high, low = halves(jnp.concatenate(blocks, axis=0).T)
+        return dot(jnp.concatenate([high, low], axis=1), spread_back[pair, side])
+
+    pairs = chunks // 2
+    for pair in range(pairs):
+        for chunk in (2 * pair, 2 * pair + 1):
+            out_copy(chunk, 0).wait()
+            all_of(back.at[chunk, 1:], got_out.at[chunk])
+        if pair < pairs - 1:
+            for side in range(2):
+
+                def settle(tile, carry):
+                    column = pl.multiple_of(tile * lanes, lanes)
+                    turned[side * half_tiles + tile] += change(pair, side, column)
+                    return carry
+
+                lax.fori_loop(0, half_tiles, settle, 0)
         else:
-            lax.fori_loop(0, full, settle, 0)
-        if rest:
-            if chunk == 0:
-                out_ref[full * lanes :, :] = (two_ref[full].T + change(full))[:rest]
-            else:
-                out_ref[full * lanes :, :] += change(full)[:rest]
-        for n in range(1, parts):
-            out_copy(chunk, n).wait_send()
+            for tile in range(tiles):
+                side, column = divmod(tile, half_tiles)
+                size = min(lanes, width - tile * lanes)
+                if size > 0:
+                    value = turned[tile] + change(pair, side, column * lanes)
+                    out_ref[tile * lanes : tile * lanes + size, :] = value[:size]
+    all_of(result.at[chunks - 1, 1:], sent_out.at[chunks - 1])
 
 
 def fused_tables(width):
@@ -944,7 +975,8 @@
     tiles = 2 * pl.cdiv(width, 2 * LANES)
     wide = tiles * LANES
     each = ACT // parts
-    chunks = each // GROUP
+    chunks = each // HALF
+    assert gain_first.shape[0] % 2 == 0
     terms = gain_first.shape[0]
     depth = pl.cdiv(3 * plane, 256) * 256
     smem, f32, bf16 = pltpu.SMEM, jnp.float32, jnp.bfloat16
@@ -961,21 +993,23 @@
         + [pltpu.VMEM(gain_first.shape, f32)] * 2
         + [pltpu.VMEM((loss_rates.size // LANES, LANES), f32)]
         + [pltpu.VMEM(planes.shape, bf16), pltpu.VMEM(speed.shape, f32)]
-        + [pltpu.VMEM((tiles, count, LANES), f32)] * 3
+        + [pltpu.VMEM((tiles, count, LANES), f32)] * 2
+        + [pltpu.VMEM((count, LANES), f32), pltpu.VMEM((tiles, LANES, count), f32)]
         + [pltpu.VMEM((count, LANES), f32)] * 3
         + [pltpu.VMEM((tiles, 8, LANES), f32)]
         + [strips] * 3
-        + [pltpu.VMEM((ACT, 2 * count), bf16), pltpu.VMEM((chunks, 2 * parts * GROUP, count), bf16)]
+        + [pltpu.VMEM((ACT, 2 * count), bf16), pltpu.VMEM((chunks // 2, 2, 4 * parts * GROUP, count), bf16)]
         + [pltpu.VMEM((depth, plane), bf16)]
         + [pltpu.VMEM((VDIM, terms, plane), f32)] * 2
-        + [pltpu.VMEM((VDIM, plane), f32)]
+        + [pltpu.VMEM((terms, VDIM, GROUP, plane), f32), pltpu.VMEM((VDIM, plane), f32)]
         + [pltpu.VMEM((2 * VDIM * GROUP, depth), bf16), pltpu.VMEM((2 * VDIM * GROUP, plane), f32)]
-        + [pltpu.VMEM((VDIM * GROUP, plane), f32)] * 2
+        + [pltpu.VMEM((VDIM * GROUP, plane), f32)] * 4
+        + [pltpu.VMEM((parts, GROUP, wide), f32)]
         + [pltpu.VMEM((tiles // 2, parts, each, 2 * LANES), f32), pltpu.VMEM((parts, each, wide), f32)]
-        + [pltpu.VMEM((chunks, parts, GROUP, wide), f32)] * 2
+        + [pltpu.VMEM((chunks, parts, GROUP, wide // 2), f32)] * 2
         + [dma((2, tiles))] * 4
-        + [dma((tiles // 2, parts)), dma((tiles // 2, parts)), dma((tiles // 2,))]
-        + [dma((chunks, parts)), dma((chunks, parts)), dma((chunks,)), dma((2,)), dma((8,))],
+        + [dma((tiles // 2,))] * 3
+        + [dma((chunks,))] * 3 + [dma((2,)), dma((8,))],
         compiler_params=pltpu.CompilerParams(
             collective_id=2, has_side_effects=True, vmem_limit_bytes=56 * 1024 * 1024
         ),

time: 73.6 us -> 69.2 us (0.940)
  Pallas kernels: 71.3 us -> 67.2 us
    pallas_call x1, Pallas kernels: 71.3 us -> 67.2 us  [fused(): pl.pallas_call(fused_kernel, in_specs=[pl.BlockSpec(memory_space=pltpu.HB...]
where the time goes in v3:
time: 69.2 us; the launch traced here: 69.1 us
  Pallas kernels  67.2 us (97%)
  local copies, waits for them, and re-layouts  1.21 us (2%)
    pallas_call x1, Pallas kernels, fused(): pl.pallas_call(fused_kernel, in_specs=[pl.BlockSpec(memory_space=pltpu.HB...  67.2 us

profile of v3, /device:TPU:1, one launch (start us, length us, event | category | flops | bytes accessed | tf_op | source)
XLA Modules:
  0.0 69.1 jit_solution(15245831329164065487)
XLA Ops:
  0.7 67.2 %shard_map.91 = f32[1728,256]{1,0:T(8,128)S(1)} custom-call(s32[1,4]{1,0:T(1,128)} %near_hbm.1, s32[1]{0:T(128)S(6)} %copy.12.level_hbm, f32[1728,256]{1,0:T(8,128)} %bitcast.9, s32[1,256]{1,0:T(1,128)} %bitcast.11, f32[6,13824]{1,0:T(8,128)} %first_hbm.1, f32[6,13824]{1,0:T(8,128)} %second_hbm.1, f32[108,128]{1,0:T(8,128)} %bitcast.10, ...), custom_call_target="tpu_custom_call" | custom-call | tf_op jit(solution)/shard_map/pallas_call | solution.py:986
  67.9 1.2 %copy.11 = f32[1,256,1728]{1,2,0:T(8,128)} copy(f32[1,256,1728]{1,2,0:T(8,128)S(1)} %bitcast.8) | data formatting | bytes 3538944

commit v4 on v3

--- a/solution.py
+++ b/solution.py
@@ -88,7 +88,7 @@
         before = edge
 
 
-def advance(source_ref, ratio, u_ref, base_ref, left_ref, right_ref, speed_ref, out_ref, fluxes):
+def advance(source_ref, ratio, u_ref, base_ref, edge_of, speed_ref, out_ref, fluxes):
     side = BSIDE
     lanes = u_ref.shape[1]
     flux_one, flux_two, flux_turned = fluxes
@@ -100,11 +100,10 @@
         return u_ref[pl.ds(n, side, stride=side), :]
 
     def ghost(face, block, own):
-        at = block * side
         return (
-            source_ref[3 * face] * left_ref[at : at + side]
+            source_ref[3 * face] * edge_of(0, block)
             + source_ref[3 * face + 1] * own
-            + source_ref[3 * face + 2] * right_ref[at : at + side]
+            + source_ref[3 * face + 2] * edge_of(1, block)
         )
 
     def padded(line, faces, start):
@@ -139,6 +138,10 @@
 
 def against_masks(speed_ref):
     return spread(speed_ref, 2) > 0.5, spread(speed_ref, 3) > 0.5
+
+
+def plain_edges(left_ref, right_ref):
+    return lambda n, block: (left_ref, right_ref)[n][block * BSIDE : (block + 1) * BSIDE]
 
 
 def transport_kernel(
@@ -218,7 +221,7 @@
     def first(tile, carry):
         receive(0, tile)
         advance(
-            source_ref, ratio, u_ref.at[tile], None, from_left.at[0, tile], from_right.at[0, tile],
+            source_ref, ratio, u_ref.at[tile], None, plain_edges(from_left.at[0, tile], from_right.at[0, tile]),
             speed_ref.at[tile], one_ref.at[tile], fluxes,
         )
         send(1, tile, one_ref)
@@ -229,7 +232,7 @@
     def second(tile, carry):
         receive(1, tile)
         advance(
-            source_ref, ratio, one_ref.at[tile], u_ref.at[tile], from_left.at[1, tile], from_right.at[1, tile],
+            source_ref, ratio, one_ref.at[tile], u_ref.at[tile], plain_edges(from_left.at[1, tile], from_right.at[1, tile]),
             speed_ref.at[tile], out_ref.at[tile], fluxes,
         )
         return carry
@@ -547,11 +550,47 @@
 AHEAD = 3
 
 
+INSET = 2
+INNER = BSIDE - 2 * INSET
+STRIP = -(-(5 * BSIDE + 5 * INNER) // GROUP) * GROUP
+
+
+def pack_edges(cells_ref, against_first, against_second, strips_ref):
+    side = BSIDE
+
+    def first(n):
+        return cells_ref[n * side : (n + 1) * side]
+
+    def second(n):
+        return cells_ref[pl.ds(n + INSET * side, INNER, stride=side), :]
+
+    at = 0
+    for line, against, size in ((first, against_first, side), (second, against_second[:INNER], INNER)):
+        far = jnp.where(against, line(2), line(side - 3))
+        for layer in (line(0), line(1), far, line(side - 2), line(side - 1)):
+            strips_ref[at : at + size] = layer
+            at += size
+
+
+def unpack_edges(strips_ref, against_second, edges_ref):
+    side = BSIDE
+    for n, at in enumerate((0, 1, None, side - 2, side - 1)):
+        inner = 5 * side + n * INNER
+        edges_ref[n, INSET : INSET + INNER] = strips_ref[inner : inner + INNER]
+        for rows, layer in ((0, 0), (side - INSET, 3)):
+            if at is None:
+                ends = [strips_ref[pl.ds(layer * side + j, INSET, stride=side), :] for j in (2, side - 3)]
+                value = jnp.where(against_second[:INSET], ends[0], ends[1])
+            else:
+                value = strips_ref[pl.ds(layer * side + at, INSET, stride=side), :]
+            edges_ref[n, rows : rows + INSET] = value
+
+
 def fused_kernel(
     near_hbm, level_hbm, x_hbm, mask_hbm, first_hbm, second_hbm, loss_hbm, plane_hbm, speed_hbm, out_ref,
     near_ref, level_ref, x_ref, mask_ref, first_ref, second_ref, loss_ref, plane_ref, speed_ref,
     u_ref, one_ref, two_ref, turned, flux_one, flux_two, flux_turned, speeds, strips, from_left, from_right,
-    pick, spread_back, table, first_cube, second_cube, gains, loss_cube, lhs, mapped, spectrum, doubled, loss, total, flat,
+    pick, spread_back, table, first_cube, second_cube, gains, loss_cube, lhs, mapped, spectrum, doubled, loss, total, flat, edges,
     sent, got, result, back,
     sent_left, sent_right, got_left, got_right, sent_in, got_in, own_in, sent_out, got_out, own_out,
     x_here, here,
@@ -633,7 +672,7 @@
         )
 
     def send(turn, tile, cells_ref):
-        pack_strips(cells_ref.at[tile], *against_masks(speeds.at[tile]), strips.at[turn, tile])
+        pack_edges(cells_ref.at[tile], *against_masks(speeds.at[tile]), strips.at[turn, tile])
 
         @pl.when(has_right)
         def _():
@@ -746,10 +785,37 @@
             device_id={"vel": peers[n]}, device_id_type=mesh_ids,
         )
 
+    def ghosts(turn, tile):
+        whole = (from_left.at[turn, tile], from_right.at[turn, tile])
+        against = against_masks(speeds.at[tile])[1]
+        for n in range(2):
+            unpack_edges(whole[n], against, edges.at[turn, n])
+
+        def edge(n, block):
+            if block < 5:
+                return whole[n][block * BSIDE : (block + 1) * BSIDE]
+            return edges[turn, n, block - 5]
+
+        return edge
+
+    def single_copy(tile, n):
+        lane = pl.ds(tile * lanes, lanes)
+        at = tile % 2 * lanes
+        place = tiles // 2 - 1 + tile % 2
+        if n == 0:
+            return pltpu.make_async_copy(
+                sent.at[tile // 2, me, :, at : at + lanes], got.at[me, :, lane], own_in.at[place]
+            )
+        return pltpu.make_async_remote_copy(
+            src_ref=sent.at[tile // 2, peers[n], :, at : at + lanes], dst_ref=got.at[me, :, lane],
+            send_sem=sent_in.at[place], recv_sem=got_in.at[place],
+            device_id={"vel": peers[n]}, device_id_type=mesh_ids,
+        )
+
     def first(tile):
         receive(0, tile)
         advance(
-            source, ratio, u_ref.at[tile], None, from_left.at[0, tile], from_right.at[0, tile],
+            source, ratio, u_ref.at[tile], None, ghosts(0, tile),
             speeds.at[tile], one_ref.at[tile], fluxes,
         )
         send(1, tile, one_ref)
@@ -757,19 +823,24 @@
     def second(tile):
         receive(1, tile)
         advance(
-            source, ratio, one_ref.at[tile], u_ref.at[tile], from_left.at[1, tile], from_right.at[1, tile],
+            source, ratio, one_ref.at[tile], u_ref.at[tile], ghosts(1, tile),
             speeds.at[tile], two_ref, fluxes,
         )
         turned[tile] = two_ref[...].T
         high, low = halves(two_ref[...])
         picked = dot(pick[...], jnp.concatenate([high, low], axis=0)).reshape(parts, each, lanes)
-        side = lax.rem(tile, 2)
-        sent[tile // 2, :, :, pl.ds(pl.multiple_of(side * lanes, lanes), lanes)] = picked
-
-        @pl.when(side == 1)
-        def _():
+        side = tile % 2 if isinstance(tile, int) else lax.rem(tile, 2)
+        sent[tile // 2, :, :, pl.ds(side * lanes if isinstance(tile, int) else pl.multiple_of(side * lanes, lanes), lanes)] = picked
+
+        if isinstance(tile, int):
             for n in range(parts):
-                in_copy(tile // 2, n).start()
+                single_copy(tile, n).start()
+        else:
+
+            @pl.when(side == 1)
+            def _():
+                for n in range(parts):
+                    in_copy(tile // 2, n).start()
 
     def early(tile, carry):
         launch(tile + AHEAD)
@@ -785,20 +856,20 @@
         second(tile - LAG)
         return carry
 
-    def late(tile, carry):
-        second(tile)
-        return carry
-
     lax.fori_loop(0, LAG, early, 0)
     lax.fori_loop(LAG, tiles, steady, 0)
-    lax.fori_loop(tiles - LAG, tiles, late, 0)
+    for tile in range(tiles - LAG, tiles):
+        second(tile)
 
     def arrive(tile, carry):
         in_copy(tile, 0).wait()
         all_of(got.at[1:, :, pl.ds(pl.multiple_of(tile * 2 * lanes, 2 * lanes), 2 * lanes)], got_in.at[tile])
         return carry
 
-    lax.fori_loop(0, tiles // 2, arrive, 0)
+    lax.fori_loop(0, tiles // 2 - 1, arrive, 0)
+    for tile in range(tiles - 2, tiles):
+        single_copy(tile, 0).wait()
+        all_of(got.at[1:, :, tile * lanes : (tile + 1) * lanes], got_in.at[tiles // 2 - 1 + tile % 2])
 
     def write_lhs(at, value):
         high, low = halves(value)
@@ -914,7 +985,10 @@
         all_of(sent.at[pair, 1:], sent_in.at[pair])
         return carry
 
-    lax.fori_loop(0, tiles // 2, inward_sent, 0)
+    lax.fori_loop(0, tiles // 2 - 1, inward_sent, 0)
+    for tile in range(tiles - 2, tiles):
+        at = tile % 2 * lanes
+        all_of(sent.at[tiles // 2 - 1, 1:, :, at : at + lanes], sent_in.at[tiles // 2 - 1 + tile % 2])
 
     half_tiles = tiles // 2
     for chunk in range(chunks - 1):
@@ -981,7 +1055,7 @@
     depth = pl.cdiv(3 * plane, 256) * 256
     smem, f32, bf16 = pltpu.SMEM, jnp.float32, jnp.bfloat16
     speed, planes = fused_tables(width)
-    strips = pltpu.VMEM((2, tiles, 10 * BSIDE, LANES), f32)
+    strips = pltpu.VMEM((2, tiles, STRIP, LANES), f32)
     dma = pltpu.SemaphoreType.DMA
     return pl.pallas_call(
         fused_kernel,
@@ -1004,11 +1078,11 @@
         + [pltpu.VMEM((terms, VDIM, GROUP, plane), f32), pltpu.VMEM((VDIM, plane), f32)]
         + [pltpu.VMEM((2 * VDIM * GROUP, depth), bf16), pltpu.VMEM((2 * VDIM * GROUP, plane), f32)]
         + [pltpu.VMEM((VDIM * GROUP, plane), f32)] * 4
-        + [pltpu.VMEM((parts, GROUP, wide), f32)]
+        + [pltpu.VMEM((parts, GROUP, wide), f32), pltpu.VMEM((2, 2, 5, BSIDE, LANES), f32)]
         + [pltpu.VMEM((tiles // 2, parts, each, 2 * LANES), f32), pltpu.VMEM((parts, each, wide), f32)]
         + [pltpu.VMEM((chunks, parts, GROUP, wide // 2), f32)] * 2
         + [dma((2, tiles))] * 4
-        + [dma((tiles // 2,))] * 3
+        + [dma((tiles // 2 + 1,))] * 3
         + [dma((chunks,))] * 3 + [dma((2,)), dma((8,))],
         compiler_params=pltpu.CompilerParams(
             collective_id=2, has_side_effects=True, vmem_limit_bytes=56 * 1024 * 1024

time: 69.2 us -> 67.2 us (0.971)
  Pallas kernels: 67.2 us -> 64.6 us
    pallas_call x1, Pallas kernels: 67.2 us -> 64.6 us  [fused(): pl.pallas_call(fused_kernel, in_specs=[pl.BlockSpec(memory_space=pltpu.HB...]
where the time goes in v4:
time: 67.2 us; the launch traced here: 66.5 us
  Pallas kernels  64.6 us (96%)
  local copies, waits for them, and re-layouts  1.21 us (2%)
    pallas_call x1, Pallas kernels, fused(): pl.pallas_call(fused_kernel, in_specs=[pl.BlockSpec(memory_space=pltpu.HB...  64.6 us

profile of v4, /device:TPU:1, one launch (start us, length us, event | category | flops | bytes accessed | tf_op | source)
XLA Modules:
  0.0 66.5 jit_solution(6248402221883710365)
XLA Ops:
  0.7 64.6 %shard_map.91 = f32[1728,256]{1,0:T(8,128)S(1)} custom-call(s32[1,4]{1,0:T(1,128)} %near_hbm.1, s32[1]{0:T(128)S(6)} %copy.12.level_hbm, f32[1728,256]{1,0:T(8,128)} %bitcast.9, s32[1,256]{1,0:T(1,128)} %bitcast.11, f32[6,13824]{1,0:T(8,128)} %first_hbm.1, f32[6,13824]{1,0:T(8,128)} %second_hbm.1, f32[108,128]{1,0:T(8,128)} %bitcast.10, ...), custom_call_target="tpu_custom_call" | custom-call | tf_op jit(solution)/shard_map/pallas_call | solution.py:1060
  65.2 1.2 %copy.11 = f32[1,256,1728]{1,2,0:T(8,128)} copy(f32[1,256,1728]{1,2,0:T(8,128)S(1)} %bitcast.8) | data formatting | bytes 3538944

commit v5 on v4

--- a/solution.py
+++ b/solution.py
@@ -608,6 +608,7 @@
     has_left, has_right = row > 0, row < rows - 1
     left, right = lax.rem(row + rows - 1, rows), lax.rem(row + 1, rows)
     peers = [lax.rem(me + n, parts) for n in range(parts)]
+    order_of = sorted(range(parts), key=lambda n: abs(n - parts // 2) if n else -1)
     mesh_ids = pl.DeviceIdType.MESH
     fluxes = (flux_one, flux_two, flux_turned)
 
@@ -776,7 +777,7 @@
         pltpu.make_async_copy(ref, ref, sem).wait()
 
     def in_copy(tile, n):
-        lane = pl.ds(pl.multiple_of(tile * 2 * lanes, 2 * lanes), 2 * lanes)
+        lane = pl.ds(pl.multiple_of(tile * lanes, lanes), lanes)
         if n == 0:
             return pltpu.make_async_copy(sent.at[tile, me], got.at[me, :, lane], own_in.at[tile])
         return pltpu.make_async_remote_copy(
@@ -784,6 +785,19 @@
             send_sem=sent_in.at[tile], recv_sem=got_in.at[tile],
             device_id={"vel": peers[n]}, device_id_type=mesh_ids,
         )
+
+    def ghosts(turn, tile):
+        whole = (from_left.at[turn, tile], from_right.at[turn, tile])
+        against = against_masks(speeds.at[tile])[1]
+        for n in range(2):
+            unpack_edges(whole[n], against, edges.at[turn, n])
+
+        def edge(n, block):
+            if block < 5:
+                return whole[n][block * BSIDE : (block + 1) * BSIDE]
+            return edges[turn, n, block - 5]
+
+        return edge
 
     def ghosts(turn, tile):
         whole = (from_left.at[turn, tile], from_right.at[turn, tile])
@@ -828,19 +842,9 @@
         )
         turned[tile] = two_ref[...].T
         high, low = halves(two_ref[...])
-        picked = dot(pick[...], jnp.concatenate([high, low], axis=0)).reshape(parts, each, lanes)
-        side = tile % 2 if isinstance(tile, int) else lax.rem(tile, 2)
-        sent[tile // 2, :, :, pl.ds(side * lanes if isinstance(tile, int) else pl.multiple_of(side * lanes, lanes), lanes)] = picked
-
-        if isinstance(tile, int):
-            for n in range(parts):
-                single_copy(tile, n).start()
-        else:
-
-            @pl.when(side == 1)
-            def _():
-                for n in range(parts):
-                    in_copy(tile // 2, n).start()
+        sent[tile] = dot(pick[...], jnp.concatenate([high, low], axis=0)).reshape(parts, each, lanes)
+        for n in order_of:
+            in_copy(tile, n).start()
 
     def early(tile, carry):
         launch(tile + AHEAD)
@@ -856,20 +860,20 @@
         second(tile - LAG)
         return carry
 
+    def late(tile, carry):
+        second(tile)
+        return carry
+
     lax.fori_loop(0, LAG, early, 0)
     lax.fori_loop(LAG, tiles, steady, 0)
-    for tile in range(tiles - LAG, tiles):
-        second(tile)
+    lax.fori_loop(tiles - LAG, tiles, late, 0)
 
     def arrive(tile, carry):
         in_copy(tile, 0).wait()
-        all_of(got.at[1:, :, pl.ds(pl.multiple_of(tile * 2 * lanes, 2 * lanes), 2 * lanes)], got_in.at[tile])
-        return carry
-
-    lax.fori_loop(0, tiles // 2 - 1, arrive, 0)
-    for tile in range(tiles - 2, tiles):
-        single_copy(tile, 0).wait()
-        all_of(got.at[1:, :, tile * lanes : (tile + 1) * lanes], got_in.at[tiles // 2 - 1 + tile % 2])
+        all_of(got.at[1:, :, pl.ds(pl.multiple_of(tile * lanes, lanes), lanes)], got_in.at[tile])
+        return carry
+
+    lax.fori_loop(0, tiles, arrive, 0)
 
     def write_lhs(at, value):
         high, low = halves(value)
@@ -985,10 +989,7 @@
         all_of(sent.at[pair, 1:], sent_in.at[pair])
         return carry
 
-    lax.fori_loop(0, tiles // 2 - 1, inward_sent, 0)
-    for tile in range(tiles - 2, tiles):
-        at = tile % 2 * lanes
-        all_of(sent.at[tiles // 2 - 1, 1:, :, at : at + lanes], sent_in.at[tiles // 2 - 1 + tile % 2])
+    lax.fori_loop(0, tiles, inward_sent, 0)
 
     half_tiles = tiles // 2
     for chunk in range(chunks - 1):
@@ -1079,10 +1080,10 @@
         + [pltpu.VMEM((2 * VDIM * GROUP, depth), bf16), pltpu.VMEM((2 * VDIM * GROUP, plane), f32)]
         + [pltpu.VMEM((VDIM * GROUP, plane), f32)] * 4
         + [pltpu.VMEM((parts, GROUP, wide), f32), pltpu.VMEM((2, 2, 5, BSIDE, LANES), f32)]
-        + [pltpu.VMEM((tiles // 2, parts, each, 2 * LANES), f32), pltpu.VMEM((parts, each, wide), f32)]
+        + [pltpu.VMEM((tiles, parts, each, LANES), f32), pltpu.VMEM((parts, each, wide), f32)]
         + [pltpu.VMEM((chunks, parts, GROUP, wide // 2), f32)] * 2
         + [dma((2, tiles))] * 4
-        + [dma((tiles // 2 + 1,))] * 3
+        + [dma((tiles,))] * 3
         + [dma((chunks,))] * 3 + [dma((2,)), dma((8,))],
         compiler_params=pltpu.CompilerParams(
             collective_id=2, has_side_effects=True, vmem_limit_bytes=56 * 1024 * 1024

time: 67.2 us -> 67.3 us (level)
  no operation moved by 1% of the time
where the time goes in v5:
time: 67.3 us; the launch traced here: 66.4 us
  Pallas kernels  64.5 us (96%)
  local copies, waits for them, and re-layouts  1.21 us (2%)
    pallas_call x1, Pallas kernels, fused(): pl.pallas_call(fused_kernel, in_specs=[pl.BlockSpec(memory_space=pltpu.HB...  64.5 us

profile of v5, /device:TPU:1, one launch (start us, length us, event | category | flops | bytes accessed | tf_op | source)
XLA Modules:
  0.0 66.4 jit_solution(3770365241248595782)
XLA Ops:
  0.7 64.5 %shard_map.91 = f32[1728,256]{1,0:T(8,128)S(1)} custom-call(s32[1,4]{1,0:T(1,128)} %near_hbm.1, s32[1]{0:T(128)S(6)} %copy.12.level_hbm, f32[1728,256]{1,0:T(8,128)} %bitcast.9, s32[1,256]{1,0:T(1,128)} %bitcast.11, f32[6,13824]{1,0:T(8,128)} %first_hbm.1, f32[6,13824]{1,0:T(8,128)} %second_hbm.1, f32[108,128]{1,0:T(8,128)} %bitcast.10, ...), custom_call_target="tpu_custom_call" | custom-call | tf_op jit(solution)/shard_map/pallas_call | solution.py:1061
  65.2 1.2 %copy.11 = f32[1,256,1728]{1,2,0:T(8,128)} copy(f32[1,256,1728]{1,2,0:T(8,128)S(1)} %bitcast.8) | data formatting | bytes 3538944
